TPU v7x, 256 devices: a whole 4x4x8 slice. The times are simulated.
256 devices in a mesh: dom: 32 (over x, z), grp: 8 (over y, core).
Axes of the slice: x: 4, y: 4, z: 8, core: 2. Of those that a mesh axis runs over, the one named last changes fastest.
Arguments:
- node_feats: bfloat16 [65536, 1024], P(('dom', 'grp')), may hold values from -6 to 6
- weight: bfloat16 [1024, 512], replicated, may hold values from -0.1875 to 0.1875
- bias: float32 [512], replicated, may hold values from -4 to 4
- cotangent: bfloat16 [65536, 512], P(('dom', 'grp')), may hold values from -6 to 6
- tile_bank: bfloat16 [16, 128, 128], replicated, may hold values from -0.125 to 0.125
- local_cols: int32 [32, 16, 16], P('dom'), may hold values from 0 to 15
- local_banks: int32 [32, 16, 16], P('dom'), may hold values from 0 to 15
- published: int32 [32, 4], P('dom'), may hold values from 0 to 15, as said below
- send_table: int32 [32, 32, 2], replicated, may hold values from -1 to 3, as said below
- halo_rows: int32 [32, 32, 2], P('dom'), may hold values from 0 to 15
- halo_banks: int32 [32, 32, 2], P('dom'), may hold values from 0 to 15
Outputs:
- activations: bfloat16 [65536, 512], P(('dom', 'grp'))
- grad_nodes: bfloat16 [65536, 1024], P(('dom', 'grp'))
- grad_weight: float32 [1024, 512], replicated
- grad_bias: float32 [512], replicated
Inputs may be any that keep to these rules, and one draw needn't show every extreme that they name: `published`: the 4 entries of a partition are distinct block numbers of that partition; 0 and 15 each appear in some partition's list. `send_table`: entry s of the pair (src, p) is -1 or an index into the offered list of src; the live entries of a pair come first and are distinct; a pair (p, p) has none; some pair has all 2 entries live.
All inputs are finite; a program needn't handle non-finite values.
Results may differ from a plain program's by a relative error of at most 0.019.
The roundings to bfloat16 on the way count: a program that leaves them out, or rounds other values in their place, can miss the bound.
Values may be sent and summed in bfloat16 or wider, within the bound.
A program may use at most 64 MiB of HBM per device.

v0:
```python
import jax
import jax.numpy as jnp
from jax import lax
from jax.sharding import PartitionSpec as P


def per_device(
    node_feats,
    weight,
    bias,
    cotangent,
    tile_bank,
    local_cols,
    local_banks,
    published,
    send_table,
    halo_rows,
    halo_banks,
):
    domains = lax.axis_size("dom")
    groups = lax.axis_size("grp")
    domain_index = lax.axis_index("dom")
    rows_here = node_feats.shape[0]
    tile_size = tile_bank.shape[1]
    slot_count = send_table.shape[2]
    pub_count = published.shape[1]
    tiles_row = local_cols.shape[2]
    features = lax.all_to_all(node_feats, "grp", split_axis=1, concat_axis=0, tiled=True)
    part_rows, narrow = features.shape
    blocks = part_rows // tile_size
    feat_blocks = features.reshape(blocks, tile_size, narrow)
    cols_here = local_cols[0]
    banks_here = local_banks[0]
    own_pub = published[0]
    incoming = lax.dynamic_index_in_dim(send_table, domain_index, 1, keepdims=False)
    live_in = (incoming >= 0).astype(jnp.float32)[:, :, None, None]
    rows_in = halo_rows[0]
    halo_tiles = tile_bank[halo_banks[0]]
    source_ids = lax.broadcasted_iota(jnp.int32, (domains, slot_count), 0)
    gathered_ids = source_ids * pub_count + jnp.maximum(incoming, 0)

    def forward_tiles(position, running):
        column = lax.dynamic_index_in_dim(cols_here, position, 1, keepdims=False)
        bank_ids = lax.dynamic_index_in_dim(banks_here, position, 1, keepdims=False)
        return running + jnp.einsum(
            "rij,rjf->rif",
            tile_bank[bank_ids],
            feat_blocks[column],
            preferred_element_type=jnp.float32,
        )

    running = lax.fori_loop(
        0, tiles_row, forward_tiles, jnp.zeros((blocks, tile_size, narrow), jnp.float32)
    )
    shared = feat_blocks[own_pub]
    everyone = lax.all_gather(shared, "dom", axis=0, tiled=True)
    remote = everyone[gathered_ids]
    halo_terms = (
        jnp.einsum("dsij,dsjf->dsif", halo_tiles, remote, preferred_element_type=jnp.float32)
        * live_in
    )
    running = running + jax.ops.segment_sum(
        halo_terms.reshape(domains * slot_count, tile_size, narrow),
        rows_in.reshape(-1),
        num_segments=blocks,
    )
    agg_narrow = running.astype(jnp.bfloat16).reshape(part_rows, narrow)
    aggregated = lax.all_to_all(agg_narrow, "grp", split_axis=0, concat_axis=1, tiled=True)
    pre_act = jnp.dot(aggregated, weight, preferred_element_type=jnp.float32) + bias
    activations = jnp.maximum(pre_act, 0.0).astype(jnp.bfloat16)
    grad_pre = jnp.where(pre_act > 0, cotangent.astype(jnp.float32), 0.0).astype(jnp.bfloat16)
    weight_part = lax.dot_general(
        aggregated, grad_pre, (((0,), (0,)), ((), ())), preferred_element_type=jnp.float32
    )
    bias_part = jnp.sum(grad_pre.astype(jnp.float32), axis=0)
    grad_agg = lax.dot_general(
        grad_pre, weight, (((1,), (1,)), ((), ())), preferred_element_type=jnp.float32
    ).astype(jnp.bfloat16)
    grad_narrow = lax.all_to_all(grad_agg, "grp", split_axis=1, concat_axis=0, tiled=True)
    grad_blocks = grad_narrow.reshape(blocks, tile_size, narrow)

    def backward_tiles(position, running):
        column = lax.dynamic_index_in_dim(cols_here, position, 1, keepdims=False)
        bank_ids = lax.dynamic_index_in_dim(banks_here, position, 1, keepdims=False)
        contrib = jnp.einsum(
            "rji,rjf->rif", tile_bank[bank_ids], grad_blocks, preferred_element_type=jnp.float32
        )
        return running + jax.ops.segment_sum(contrib, column, num_segments=blocks)

    grad_total = lax.fori_loop(
        0, tiles_row, backward_tiles, jnp.zeros((blocks, tile_size, narrow), jnp.float32)
    )
    back_terms = (
        jnp.einsum(
            "dsji,dsjf->dsif", halo_tiles, grad_blocks[rows_in], preferred_element_type=jnp.float32
        )
        * live_in
    )
    placed = jax.ops.segment_sum(
        back_terms.reshape(domains * slot_count, tile_size, narrow),
        gathered_ids.reshape(-1),
        num_segments=domains * pub_count,
    )
    mine_back = lax.psum_scatter(placed, "dom", scatter_dimension=0, tiled=True)
    back_total = jax.ops.segment_sum(mine_back, own_pub, num_segments=blocks)
    grad_total = grad_total + back_total
    grad_nodes = lax.all_to_all(
        grad_total.astype(jnp.bfloat16).reshape(part_rows, narrow),
        "grp",
        split_axis=0,
        concat_axis=1,
        tiled=True,
    )
    norm_scale = float(rows_here * groups * domains) ** (-0.5)
    weight_total, bias_total = lax.psum((weight_part, bias_part), ("dom", "grp"))
    return (activations, grad_nodes, weight_total * norm_scale, bias_total * norm_scale)


def solution(mesh):
    in_specs = (
        P(("dom", "grp"), None),
        P(),
        P(),
        P(("dom", "grp"), None),
        P(),
        P("dom", None, None),
        P("dom", None, None),
        P("dom", None),
        P(),
        P("dom", None, None),
        P("dom", None, None),
    )
    out_specs = (P(("dom", "grp"), None), P(("dom", "grp"), None), P(), P())
    return jax.shard_map(
        per_device, mesh=mesh, in_specs=in_specs, out_specs=out_specs, check_vma=False
    )
```

profile of v0, /device:TPU:1, one launch (start us, length us, event | category | flops | bytes accessed | tf_op | source)
XLA Modules:
  0.0 686.6 jit_solution(15913844381797116386)
XLA Ops:
  9.3 7.3 %all-to-all-start = ((bf16[256,8,128]{2,0,1:T(8,128)(2,1)}), bf16[256,8,128]{2,0,1:T(8,128)(2,1)}, u32[]{:S(2)}, u32[]{:S(2)}) async-start(bf16[256,8,128]{2,0,1:T(8,128)(2,1)} %copy_bitcast_fusion.1), calls=%async_computation | async-start | bytes 1048576 | tf_op jit(solution)/shard_map/all_to_all | solution.py:28
  19.8 6.3 all-to-all-done
  28.4 74.1 %while.28 = (s32[]{:T(128)}, f32[16,128,128]{2,1,0:T(8,128)S(1)}, s32[16,16]{0,1:T(8,128)S(1)}, bf16[16,128,128]{2,1,0:T(8,128)(2,1)S(1)}, s32[16,16]{0,1:T(8,12...) while((s32[]{:T(128)}, f32[16,128,128]{2,1,0:T(8,128)S(1)}, ...), condition=%wide.region_1.2_spmd.clone, body=%wide.region_0.1_spmd.clone.sunk | while | flops 67635296 | bytes 5251683 | solution.py:52
  102.5 5.0 all-gather.3.cloned.1.call-done
  107.5 4.3 gather_fusion.5
  111.8 4.9 convolution_multiply_fusion.1
  116.7 8.8 %scatter_fusion.1 = f32[16,128,128]{2,1,0:T(8,128)S(1)} fusion(f32[16,128,128]{2,1,0:T(8,128)S(1)} %get-tuple-element.222, s32[64]{0:T(128)S(1)} %reshape.272, f32[64,128,128]{2,1,0:T(8,128)} %bitcast.94), kind=kCustom, calls=%fused_computation.8 | custom fusion | flops 1048576 | bytes 12583168 | tf_op jit(solution)/shard_map/scatter-add | solution.py:62
  126.4 7.7 %all-to-all-start.1 = ((bf16[8,256,128]{2,1,0:T(8,128)(2,1)}), bf16[8,256,128]{2,1,0:T(8,128)(2,1)S(1)}, u32[]{:S(2)}, u32[]{:S(2)}) async-start(bf16[8,256,128]{2,1,0:T(8,128)(2,1)} %bitcast.15), calls=%async_computation.1 | async-start | bytes 1048576 | tf_op jit(solution)/shard_map/all_to_all | solution.py:68
  134.3 9.3 %all-to-all-done.1 = bf16[8,256,128]{2,1,0:T(8,128)(2,1)S(1)} async-done(((bf16[8,256,128]{2,1,0:T(8,128)(2,1)}), bf16[8,256,128]{2,1,0:T(8,128)(2,1)S(1)}, u32[]{:S(2)}, u32[]{:S(2)}) %all-to-all-start.1) | async-done | bytes 524320 | tf_op jit(solution)/shard_map/all_to_all | solution.py:68
  146.5 4.3 all-to-all-start.2
  151.2 9.1 %all-to-all-done.2 = bf16[256,8,128]{2,0,1:T(8,128)(2,1)S(1)} async-done(((bf16[256,8,128]{2,0,1:T(8,128)(2,1)}), bf16[256,8,128]{2,0,1:T(8,128)(2,1)S(1)}, u32[]{:S(2)}, u32[]{:S(2)}) %all-to-all-start.2) | async-done | bytes 524320 | tf_op jit(solution)/shard_map/all_to_all | solution.py:79
  162.4 5.2 convolution_multiply_fusion
  167.7 4.3 broadcast_in_dim.12
  171.9 13.4 %scatter_fusion.2 = f32[128,128,128]{2,1,0:T(8,128)} fusion(f32[128,128,128]{2,1,0:T(8,128)} %broadcast_in_dim.12, s32[64]{0:T(128)S(1)} %add_bitcast_fusion, f32[64,128,128]{2,1,0:T(8,128)} %bitcast.93), kind=kCustom, calls=%fused_computation.9 | custom fusion | flops 1048576 | bytes 12583168 | tf_op jit(solution)/shard_map/scatter-add | solution.py:99
  185.4 74.7 %psum.15 = f32[512]{0:T(512)S(1)} all-reduce(f32[512]{0:T(512)S(1)} %get-tuple-element.277), channel_id=1, replica_groups=mesh['dom'=32,'grp'=8] {'dom','grp'}, use_global_device_ids=true, to_apply=%region_11.12 | all-reduce | flops 512 | bytes 4096 | tf_op jit(solution)/shard_map/psum | solution.py:115
  263.0 98.4 %while.27 = (s32[]{:T(128)}, f32[16,128,128]{2,1,0:T(8,128)}, s32[16,16]{0,1:T(8,128)S(1)}, s32[16,16]{0,1:T(8,128)S(1)}, bf16[16,128,128]{2,1,0:T(8,128)(2,1)S(...) while((s32[]{:T(128)}, f32[16,128,128]{2,1,0:T(8,128)}, s32[16,16]{0,1:T(8,128)S(1)}, ...), condition=%wide.region_5.6_spmd, body=%wide.region_3.5_spmd.sunk | while | flops 67372080 | bytes 6296081 | solution.py:90
  265.8 3.3 scatter_fusion
  290.4 3.4 scatter_fusion
  296.6 3.3 scatter_fusion
  327.3 3.4 scatter_fusion
  333.5 3.3 scatter_fusion
  361.3 45.0 %reduce-scatter.2.cloned.1.call-done = f32[4,128,128]{2,1,0:T(8,128)} async-done(((f32[128,128,128]{2,1,0:T(8,128)}), f32[4,128,128]{2,1,0:T(8,128)}) %reduce-scatter.2.cloned.1.call-update) | async-done | bytes 262160 | tf_op jit(solution)/shard_map/reduce_scatter | solution.py:104
  410.9 9.2 %all-to-all-start.3 = ((bf16[8,256,128]{2,1,0:T(8,128)(2,1)}), bf16[8,256,128]{2,1,0:T(8,128)(2,1)S(1)}, u32[]{:S(2)}, u32[]{:S(2)}) async-start(bf16[8,256,128]{2,1,0:T(8,128)(2,1)} %bitcast.26), calls=%async_computation.4 | async-start | bytes 1048576 | tf_op jit(solution)/shard_map/all_to_all | solution.py:107
  420.7 255.0 %all-reduce.2.cloned.1.call-done = f32[1024,512]{1,0:T(8,128)} async-done(((f32[1024,512]{1,0:T(8,128)}), f32[1024,512]{1,0:T(8,128)}) %all-reduce.2.cloned.1.call-update) | async-done | bytes 2097168 | tf_op jit(solution)/shard_map/psum | solution.py:115
  (246 shorter events, 181.1 us)
Async XLA Ops:
  7.2 136.7 %copy-start = (bf16[1024,512]{1,0:T(8,128)(2,1)S(1)}, bf16[1024,512]{1,0:T(8,128)(2,1)}, u32[]{:S(2)}) copy-start(bf16[1024,512]{1,0:T(8,128)(2,1)} %param.16) | copy-start | bytes 3145732
  7.2 9.4 %copy-start.3 = (s32[32,32,2]{1,2,0:T(2,128)S(1)}, s32[32,32,2]{1,2,0:T(2,128)}, u32[]{:S(2)}) copy-start(s32[32,32,2]{1,2,0:T(2,128)} %param.23) | copy-start | bytes 24580
  7.2 9.6 %copy-start.8 = (s32[1,32,2]{1,2,0:T(2,128)S(1)}, s32[1,32,2]{1,2,0:T(2,128)}, u32[]{:S(2)}) copy-start(s32[1,32,2]{1,2,0:T(2,128)} %param.25) | copy-start | bytes 772
  7.2 10.1 %copy-start.4 = (s32[1,16,16]{2,1,0:T(8,128)S(1)}, s32[1,16,16]{2,1,0:T(8,128)}, u32[]{:S(2)}) copy-start(s32[1,16,16]{2,1,0:T(8,128)} %param.21) | copy-start | bytes 3076
  7.2 10.2 %copy-start.5 = (s32[1,16,16]{2,1,0:T(8,128)S(1)}, s32[1,16,16]{2,1,0:T(8,128)}, u32[]{:S(2)}) copy-start(s32[1,16,16]{2,1,0:T(8,128)} %param.20) | copy-start | bytes 3076
  7.2 10.2 %copy-start.6 = (s32[1,32,2]{1,2,0:T(2,128)S(1)}, s32[1,32,2]{1,2,0:T(2,128)}, u32[]{:S(2)}) copy-start(s32[1,32,2]{1,2,0:T(2,128)} %param.24) | copy-start | bytes 772
  7.2 10.4 %copy-start.1 = (bf16[16,128,128]{2,1,0:T(8,128)(2,1)S(1)}, bf16[16,128,128]{2,1,0:T(8,128)(2,1)}, u32[]{:S(2)}) copy-start(bf16[16,128,128]{2,1,0:T(8,128)(2,1)} %param.19) | copy-start | bytes 1572868
  9.3 16.9 %all-to-all-start = ((bf16[256,8,128]{2,0,1:T(8,128)(2,1)}), bf16[256,8,128]{2,0,1:T(8,128)(2,1)}, u32[]{:S(2)}, u32[]{:S(2)}) async-start(bf16[256,8,128]{2,0,1:T(8,128)(2,1)} %copy_bitcast_fusion.1), calls=%async_computation | async-start | bytes 1048576 | tf_op jit(solution)/shard_map/all_to_all | solution.py:28
  16.5 91.0 %all-gather.3.cloned.1.call-start = ((), (), s32[]{:S(2)}) async-start(), calls=%async_computation.7 | async-start | bytes 4325376 | tf_op jit(solution)/shard_map/all_gather | solution.py:56
  17.7 2.2 copy-start.9
  125.5 18.3 %copy-start.7 = (f32[512]{0:T(512)S(1)}, f32[512]{0:T(512)}, u32[]{:S(2)}) copy-start(f32[512]{0:T(512)} %param.17) | copy-start | bytes 6148
  126.4 18.6 %copy-start.2 = (bf16[256,512]{1,0:T(8,128)(2,1)S(1)}, bf16[256,512]{1,0:T(8,128)(2,1)}, u32[]{:S(2)}) copy-start(bf16[256,512]{1,0:T(8,128)(2,1)} %param.18) | copy-start | bytes 786436
  126.4 17.2 %all-to-all-start.1 = ((bf16[8,256,128]{2,1,0:T(8,128)(2,1)}), bf16[8,256,128]{2,1,0:T(8,128)(2,1)S(1)}, u32[]{:S(2)}, u32[]{:S(2)}) async-start(bf16[8,256,128]{2,1,0:T(8,128)(2,1)} %bitcast.15), calls=%async_computation.1 | async-start | bytes 1048576 | tf_op jit(solution)/shard_map/all_to_all | solution.py:68
  146.5 13.8 %all-to-all-start.2 = ((bf16[256,8,128]{2,0,1:T(8,128)(2,1)}), bf16[256,8,128]{2,0,1:T(8,128)(2,1)S(1)}, u32[]{:S(2)}, u32[]{:S(2)}) async-start(bf16[256,8,128]{2,0,1:T(8,128)(2,1)} %bitcast.76), calls=%async_computation.2 | async-start | bytes 1048576 | tf_op jit(solution)/shard_map/all_to_all | solution.py:79
  150.8 255.5 %reduce-scatter.2.cloned.1.call-start = ((), (), s32[]{:S(2)}) async-start(), calls=%async_computation.5 | async-start | bytes 8650752 | tf_op jit(solution)/shard_map/reduce_scatter | solution.py:104
  185.3 490.3 %all-reduce.2.cloned.1.call-start = ((), (), s32[]{:S(2)}) async-start(), calls=%async_computation.6 | async-start | bytes 4194304 | tf_op jit(solution)/shard_map/psum | solution.py:115
  410.9 268.0 %all-to-all-start.3 = ((bf16[8,256,128]{2,1,0:T(8,128)(2,1)}), bf16[8,256,128]{2,1,0:T(8,128)(2,1)S(1)}, u32[]{:S(2)}, u32[]{:S(2)}) async-start(bf16[8,256,128]{2,1,0:T(8,128)(2,1)} %bitcast.26), calls=%async_computation.4 | async-start | bytes 1048576 | tf_op jit(solution)/shard_map/all_to_all | solution.py:107
Sparse Core Ops, SparseCore 0:
  28.5 78.9 all-gather.2
  185.5 220.7 reduce-scatter.1
  413.1 262.5 all-reduce.1
where the time goes:
time: 692 us; the launch traced here: 687 us
  waiting for transfers between devices  330 us (48%)
  local copies, waits for them, and re-layouts  94.3 us (14%)
  other arithmetic  85.4 us (12%)
  blocking collectives  74.7 us (11%)
  matrix products  59 us (9%)
  starting transfers between devices  28.5 us (4%)
  between operations  14 us (2%)
    psum x1, waiting for transfers between devices, per_device(): lax.psum((weight_part, bias_part), ('dom', 'grp'))  255 us
    psum x1, blocking collectives, per_device(): lax.psum((weight_part, bias_part), ('dom', 'grp'))  74.7 us
    scatter-add x16, other arithmetic, backward_tiles(): return running + jax.ops.segment_sum(contrib, column, num_segments=blocks)  53.2 us
    reduce_scatter x1, waiting for transfers between devices, per_device(): mine_back = lax.psum_scatter(placed, 'dom', scatter_dimension=0, tiled=True)  45 us
    gather x16, local copies, waits for them, and re-layouts, forward_tiles(): feat_blocks[column]  39.2 us
    dot_general x16, matrix products, forward_tiles(): jnp.einsum('rij,rjf->rif', tile_bank[bank_ids], feat_blocks[column], pref...  23.3 us
    gather x16, local copies, waits for them, and re-layouts, backward_tiles(): tile_bank[bank_ids]  22.5 us
    dot_general x16, matrix products, backward_tiles(): jnp.einsum('rji,rjf->rif', tile_bank[bank_ids], grad_blocks, preferred_el...  22.3 us
  transfers between devices with their start and end apart: 7, of which 6 were waited for; matrix products, arithmetic and copies ran while one was open for 27% of the time, Pallas kernels for 0%

commit v1 on v0

v1 whole, which is shorter than its diff:
```python
import functools

import jax
import jax.numpy as jnp
from jax import lax
from jax.experimental import pallas as pl
from jax.experimental.pallas import tpu as pltpu
from jax.sharding import PartitionSpec as P

_SMEM = pl.BlockSpec(memory_space=pltpu.SMEM)
_VMEM = pl.BlockSpec(memory_space=pltpu.VMEM)


def _cost(matmuls, tile, nbytes):
    return pl.CostEstimate(
        flops=2 * matmuls * tile * tile * tile, transcendentals=0, bytes_accessed=nbytes
    )


def _fwd_local_kernel(cols, banks, bank_ref, feat_ref, acc_ref):
    rows, tiles = cols.shape

    def row(r, carry):
        total = jnp.zeros(acc_ref.shape[1:], jnp.float32)
        for k in range(tiles):
            total += jnp.dot(
                bank_ref[banks[r, k]], feat_ref[cols[r, k]], preferred_element_type=jnp.float32
            )
        acc_ref[r] = total
        return carry

    lax.fori_loop(0, rows, row, 0)


def _bwd_local_kernel(cols, banks, bank_t_ref, grad_ref, acc_ref):
    rows, tiles = cols.shape
    acc_ref[...] = jnp.zeros(acc_ref.shape, jnp.float32)

    def row(r, carry):
        block = grad_ref[r]
        for k in range(tiles):
            c = cols[r, k]
            acc_ref[c] += jnp.dot(
                bank_t_ref[banks[r, k]], block, preferred_element_type=jnp.float32
            )
        return carry

    lax.fori_loop(0, rows, row, 0)


def _halo_kernel(dest, banks, live, bank_ref, acc_in, blocks_ref, out_ref, acc_ref):
    acc_ref[...] = acc_in[...]

    def term(j, carry):
        @pl.when(live[j] > 0)
        def _():
            acc_ref[dest[j]] += jnp.dot(
                bank_ref[banks[j]], blocks_ref[j], preferred_element_type=jnp.float32
            )

        return carry

    lax.fori_loop(0, dest.shape[0], term, 0)
    out_ref[...] = acc_ref[...].astype(out_ref.dtype)


def _local(kernel, cols, banks, bank, blocks):
    n, tile, width = blocks.shape
    return pl.pallas_call(
        kernel,
        out_shape=jax.ShapeDtypeStruct((n, tile, width), jnp.float32),
        in_specs=[_SMEM, _SMEM, _VMEM, _VMEM],
        out_specs=_VMEM,
        cost_estimate=_cost(cols.size, tile, 2 * bank.size + 2 * blocks.size + 4 * blocks.size),
    )(cols, banks, bank, blocks)


def _halo(dest, banks, live, bank, acc, blocks):
    n, tile, width = acc.shape
    return pl.pallas_call(
        _halo_kernel,
        out_shape=jax.ShapeDtypeStruct((n, tile, width), jnp.bfloat16),
        in_specs=[_SMEM, _SMEM, _SMEM, _VMEM, _VMEM, _VMEM],
        out_specs=_VMEM,
        scratch_shapes=[pltpu.VMEM((n, tile, width), jnp.float32)],
        cost_estimate=_cost(dest.size, tile, 2 * bank.size + 6 * acc.size + 2 * blocks.size),
    )(dest, banks, live, bank, acc, blocks)


def _all_reduce(x):
    groups = lax.axis_size("grp")
    domains = lax.axis_size("dom")
    rows, width = x.shape
    chunk = -(-rows // groups)
    x = jnp.pad(x, ((0, chunk * groups - rows), (0, 0)))
    y = lax.all_to_all(x.reshape(groups, chunk, width), "grp", 0, 0, tiled=True).sum(0)
    piece = -(-chunk // domains)
    y = jnp.pad(y, ((0, piece * domains - chunk), (0, 0)))
    z = lax.all_to_all(y.reshape(domains, piece, width), "dom", 0, 0, tiled=True).sum(0)
    z = lax.all_to_all(
        jnp.broadcast_to(z[None], (domains, piece, width)), "dom", 0, 0, tiled=True
    ).reshape(domains * piece, width)[:chunk]
    z = lax.all_to_all(
        jnp.broadcast_to(z[None], (groups, chunk, width)), "grp", 0, 0, tiled=True
    ).reshape(groups * chunk, width)
    return z[:rows]


def per_device(
    node_feats,
    weight,
    bias,
    cotangent,
    tile_bank,
    local_cols,
    local_banks,
    published,
    send_table,
    halo_rows,
    halo_banks,
):
    domains = lax.axis_size("dom")
    groups = lax.axis_size("grp")
    domain_index = lax.axis_index("dom")
    rows_here = node_feats.shape[0]
    tile_size = tile_bank.shape[1]
    slot_count = send_table.shape[2]
    features = lax.all_to_all(node_feats, "grp", split_axis=1, concat_axis=0, tiled=True)
    part_rows, narrow = features.shape
    blocks = part_rows // tile_size
    feat_blocks = features.reshape(blocks, tile_size, narrow)
    cols_here = local_cols[0]
    banks_here = local_banks[0]
    own_pub = published[0]
    bank_t = jnp.swapaxes(tile_bank, 1, 2)

    outgoing = lax.dynamic_index_in_dim(send_table, domain_index, 0, keepdims=False)
    send_ids = own_pub[jnp.maximum(outgoing, 0)]
    remote = lax.all_to_all(feat_blocks[send_ids], "dom", 0, 0, tiled=True)
    incoming = lax.dynamic_index_in_dim(send_table, domain_index, 1, keepdims=False)
    live_in = (incoming >= 0).astype(jnp.int32).reshape(-1)
    rows_in = halo_rows[0]

    local_acc = _local(_fwd_local_kernel, cols_here, banks_here, tile_bank, feat_blocks)
    agg_blocks = _halo(
        rows_in.reshape(-1),
        halo_banks[0].reshape(-1),
        live_in,
        tile_bank,
        local_acc,
        remote.reshape(domains * slot_count, tile_size, narrow),
    )
    agg_narrow = agg_blocks.reshape(part_rows, narrow)
    aggregated = lax.all_to_all(agg_narrow, "grp", split_axis=0, concat_axis=1, tiled=True)
    pre_act = jnp.dot(aggregated, weight, preferred_element_type=jnp.float32) + bias
    activations = jnp.maximum(pre_act, 0.0).astype(jnp.bfloat16)
    grad_pre = jnp.where(pre_act > 0, cotangent.astype(jnp.float32), 0.0).astype(jnp.bfloat16)
    weight_part = lax.dot_general(
        aggregated, grad_pre, (((0,), (0,)), ((), ())), preferred_element_type=jnp.float32
    )
    bias_part = jnp.sum(grad_pre.astype(jnp.float32), axis=0)
    grad_agg = lax.dot_general(
        grad_pre, weight, (((1,), (1,)), ((), ())), preferred_element_type=jnp.float32
    ).astype(jnp.bfloat16)
    grad_narrow = lax.all_to_all(grad_agg, "grp", split_axis=1, concat_axis=0, tiled=True)
    grad_blocks = grad_narrow.reshape(blocks, tile_size, narrow)

    back_in = lax.all_to_all(grad_blocks[rows_in], "dom", 0, 0, tiled=True)
    banks_back = lax.all_to_all(halo_banks[0], "dom", 0, 0, tiled=True)
    live_out = (outgoing >= 0).astype(jnp.int32).reshape(-1)

    local_back = _local(_bwd_local_kernel, cols_here, banks_here, bank_t, grad_blocks)
    grad_total = _halo(
        send_ids.reshape(-1),
        banks_back.reshape(-1),
        live_out,
        bank_t,
        local_back,
        back_in.reshape(domains * slot_count, tile_size, narrow),
    )
    grad_nodes = lax.all_to_all(
        grad_total.reshape(part_rows, narrow),
        "grp",
        split_axis=0,
        concat_axis=1,
        tiled=True,
    )
    norm_scale = float(rows_here * groups * domains) ** (-0.5)
    hidden = weight_part.shape[0]
    summed = _all_reduce(jnp.concatenate([weight_part, bias_part[None]], axis=0))
    return (
        activations,
        grad_nodes,
        summed[:hidden] * norm_scale,
        summed[hidden] * norm_scale,
    )


def solution(mesh):
    in_specs = (
        P(("dom", "grp"), None),
        P(),
        P(),
        P(("dom", "grp"), None),
        P(),
        P("dom", None, None),
        P("dom", None, None),
        P("dom", None),
        P(),
        P("dom", None, None),
        P("dom", None, None),
    )
    out_specs = (P(("dom", "grp"), None), P(("dom", "grp"), None), P(), P())
    return jax.shard_map(
        per_device, mesh=mesh, in_specs=in_specs, out_specs=out_specs, check_vma=False
    )
```

time: 692 us -> 322 us (0.47)
  waiting for transfers between devices: 330 us -> 164 us
  other arithmetic: 85.4 us -> 10.9 us
  local copies, waits for them, and re-layouts: 94.3 us -> 31.7 us
  blocking collectives: 74.7 us -> 14 us
  matrix products: 59 us -> 2.06 us
  starting transfers between devices: 28.5 us -> 63.2 us
  Pallas kernels: 0 us -> 33.9 us
  between operations: 14 us -> 0.83 us
    psum x1 -> x0, waiting for transfers between devices: 255 us -> none  [per_device(): lax.psum((weight_part, bias_part), ('dom', 'grp'))]
    all_to_all x2 -> x8, waiting for transfers between devices: 9.28 us -> 149 us  [the longest x1 47.5 us: per_device(): back_in = lax.all_to_all(grad_blocks[rows_in], 'dom', 0, 0, tiled=True)]
    gather x52 -> x4, local copies, waits for them, and re-layouts: 82.9 us -> 5 us  [the longest x1 2.13 us: per_device(): back_in = lax.all_to_all(grad_blocks[rows_in], 'dom', 0, 0, tiled=True)]
    scatter-add x19 -> x0, other arithmetic: 77.9 us -> none  [the longest x16 53.2 us: backward_tiles(): return running + jax.ops.segment_sum(contrib, column, num_segments=blocks)]
    psum x1 -> x0, blocking collectives: 74.7 us -> none  [per_device(): lax.psum((weight_part, bias_part), ('dom', 'grp'))]
    dot_general x34 -> x0, matrix products: 55.6 us -> none  [the longest x16 23.3 us: forward_tiles(): jnp.einsum('rij,rjf->rif', tile_bank[bank_ids], feat_blocks[column], pref...]
    reduce_scatter x1 -> x0, waiting for transfers between devices: 45 us -> none  [per_device(): mine_back = lax.psum_scatter(placed, 'dom', scatter_dimension=0, tiled=True)]
    pallas_call x0 -> x4, Pallas kernels: none -> 33.9 us  [the longest x2 19.9 us: _halo(): pl.pallas_call(_halo_kernel, out_shape=jax.ShapeDtypeStruct((n, tile, wid...]
  transfers between devices with their start and end apart: 7 -> 10, of which waited for: 6 -> 10; matrix products, arithmetic and copies ran while one was open for 27% -> 9% of each run, Pallas kernels for 0% -> 8%
where the time goes in v1:
time: 322 us; the launch traced here: 321 us
  waiting for transfers between devices  164 us (51%)
  starting transfers between devices  63.2 us (20%)
  Pallas kernels  33.9 us (11%)
  local copies, waits for them, and re-layouts  31.7 us (10%)
  blocking collectives  14 us (4%)
  other arithmetic  10.9 us (3%)
    all_to_all x1, waiting for transfers between devices, per_device(): back_in = lax.all_to_all(grad_blocks[rows_in], 'dom', 0, 0, tiled=True)  47.5 us
    all_to_all x1, waiting for transfers between devices, per_device(): remote = lax.all_to_all(feat_blocks[send_ids], 'dom', 0, 0, tiled=True)  39 us
    all_to_all x1, waiting for transfers between devices, _all_reduce(): lax.all_to_all(x.reshape(groups, chunk, width), 'grp', 0, 0, tiled=True)  27.1 us
    pallas_call x2, Pallas kernels, _halo(): pl.pallas_call(_halo_kernel, out_shape=jax.ShapeDtypeStruct((n, tile, wid...  19.9 us
    all_to_all x1, blocking collectives, per_device(): lax.all_to_all(agg_narrow, 'grp', split_axis=0, concat_axis=1, tiled=True)  14 us
    pallas_call x2, Pallas kernels, _local(): pl.pallas_call(kernel, out_shape=jax.ShapeDtypeStruct((n, tile, width), j...  14 us
    all_to_all x1, waiting for transfers between devices, _all_reduce(): lax.all_to_all(jnp.broadcast_to(z[None], (domains, piece, width)), 'dom',...  11.7 us
    all_to_all x1, waiting for transfers between devices, _all_reduce(): lax.all_to_all(y.reshape(domains, piece, width), 'dom', 0, 0, tiled=True)  11.4 us
  transfers between devices with their start and end apart: 10, of which 10 were waited for; matrix products, arithmetic and copies ran while one was open for 9% of the time, Pallas kernels for 8%

profile of v1, /device:TPU:1, one launch (start us, length us, event | category | flops | bytes accessed | tf_op | source)
XLA Modules:
  0.0 320.6 jit_solution(17916082605710670087)
XLA Ops:
  2.7 6.6 %all-to-all-start = ((bf16[256,8,128]{2,0,1:T(8,128)(2,1)}), bf16[256,8,128]{2,0,1:T(8,128)(2,1)S(1)}, u32[]{:S(2)}, u32[]{:S(2)}) async-start(bf16[256,8,128]{2,0,1:T(8,128)(2,1)} %copy_bitcast_fusion.2), calls=%async_computation | async-start | bytes 1048576 | tf_op jit(solution)/shard_map/all_to_all | solution.py:128
  13.3 5.5 %all-to-all-done = bf16[256,8,128]{2,0,1:T(8,128)(2,1)S(1)} async-done(((bf16[256,8,128]{2,0,1:T(8,128)(2,1)}), bf16[256,8,128]{2,0,1:T(8,128)(2,1)S(1)}, u32[]{:S(2)}, u32[]{:S(2)}) %all-to-all-start) | async-done | bytes 524320 | tf_op jit(solution)/shard_map/all_to_all | solution.py:128
  21.0 10.5 %all-to-all-start.1 = ((bf16[32,2,128,128]{3,2,1,0:T(8,128)(2,1)}), bf16[32,2,128,128]{3,2,1,0:T(8,128)(2,1)S(1)}, u32[]{:S(2)}, u32[]{:S(2)}) async-start(bf16[32,2,128,128]{3,2,1,0:T(8,128)(2,1)} %bitcast.61), calls=%async_computation.1 | async-start | bytes 4194304 | tf_op jit(solution)/shard_map/all_to_all | solution.py:139
  34.3 6.9 %shard_map.138.acc_in = f32[16,128,128]{2,1,0:T(8,128)} custom-call(s32[16,16]{1,0:T(8,128)} %bitcast.72, s32[16,16]{1,0:T(8,128)} %bitcast.74, bf16[16,128,128]{2,1,0:T(8,128)(2,1)} %bank_ref.3, bf16[16,128,128]{2,1,0:T(8,128)(2,1)} %bitcast.58), custom_call_target="tpu_custom_call" | custom-call | flops 1073741824 | bytes 2097152 | tf_op jit(solution)/shard_map/pallas_call | solution.py:69
  41.2 39.0 %all-to-all-done.1 = bf16[32,2,128,128]{3,2,1,0:T(8,128)(2,1)S(1)} async-done(((bf16[32,2,128,128]{3,2,1,0:T(8,128)(2,1)}), bf16[32,2,128,128]{3,2,1,0:T(8,128)(2,1)S(1)}, u32[]{:S(2)}, u32[]{:S(2)}) %all-to-all-start.1) | async-done | bytes 2097184 | tf_op jit(solution)/shard_map/all_to_all | solution.py:139
  81.5 8.3 %shard_map.139 = bf16[16,128,128]{2,1,0:T(8,128)(2,1)} custom-call(s32[64]{0:T(128)} %reshape_squeeze.6.dest, s32[64]{0:T(128)} %reshape_squeeze.7.banks, s32[64]{0:T(128)} %reshape.140.live, bf16[16,128,128]{2,1,0:T(8,128)(2,1)} %bank_ref.3, f32[16,128,128]{2,1,0:T(8,128)} %shard_map.138.acc_in, bf16[64,128,128]{2,1,0:T(8,128)(2,1)} %bitcast.60), custom_call_target="tpu_custom_call" | custom-call | flops 268435456 | bytes 4194304 | tf_op jit(solution)/shard_map/pallas_call | solution.py:80
  91.1 14.0 %all_to_all.109 = bf16[8,256,128]{1,2,0:T(8,128)(2,1)S(1)} all-to-all(bf16[8,256,128]{1,2,0:T(8,128)(2,1)S(1)} %copy.42), channel_id=1, replica_groups=mesh['dom'=32,'grp'=8] {'grp'}, dimensions={0} | all-to-all | bytes 1048576 | tf_op jit(solution)/shard_map/all_to_all | solution.py:154
  108.7 4.5 %all-to-all-start.7 = ((f32[8,129,512]{2,1,0:T(8,128)}), f32[8,129,512]{2,1,0:T(8,128)S(1)}, u32[]{:S(2)}, u32[]{:S(2)}) async-start(f32[8,129,512]{2,1,0:T(8,128)} %reshape.136), calls=%async_computation.7 | async-start | bytes 4456448 | tf_op jit(solution)/shard_map/all_to_all | solution.py:96
  113.9 27.1 %all-to-all-done.7 = f32[8,129,512]{2,1,0:T(8,128)S(1)} async-done(((f32[8,129,512]{2,1,0:T(8,128)}), f32[8,129,512]{2,1,0:T(8,128)S(1)}, u32[]{:S(2)}, u32[]{:S(2)}) %all-to-all-start.7) | async-done | bytes 2113568 | tf_op jit(solution)/shard_map/all_to_all | solution.py:96
  141.0 5.7 %all-to-all-start.3 = ((s32[32,1,2]{2,1,0:T(1,128)}), s32[32,1,2]{2,1,0:T(1,128)S(1)}, u32[]{:S(2)}, u32[]{:S(2)}) async-start(s32[32,1,2]{2,1,0:T(1,128)} %copy.44), calls=%async_computation.3 | async-start | bytes 32768 | tf_op jit(solution)/shard_map/all_to_all | solution.py:169
  149.4 5.9 %all-to-all-done.3 = s32[32,1,2]{2,1,0:T(1,128)S(1)} async-done(((s32[32,1,2]{2,1,0:T(1,128)}), s32[32,1,2]{2,1,0:T(1,128)S(1)}, u32[]{:S(2)}, u32[]{:S(2)}) %all-to-all-start.3) | async-done | bytes 288 | tf_op jit(solution)/shard_map/all_to_all | solution.py:169
  155.3 3.9 %all-to-all-start.8 = ((f32[32,5,512]{2,1,0:T(8,128)}), f32[32,5,512]{2,1,0:T(8,128)S(1)}, u32[]{:S(2)}, u32[]{:S(2)}) async-start(f32[32,5,512]{2,1,0:T(8,128)} %reshape.137), calls=%async_computation.8 | async-start | bytes 1048576 | tf_op jit(solution)/shard_map/all_to_all | solution.py:99
  160.6 11.4 %all-to-all-done.8 = f32[32,5,512]{2,1,0:T(8,128)S(1)} async-done(((f32[32,5,512]{2,1,0:T(8,128)}), f32[32,5,512]{2,1,0:T(8,128)S(1)}, u32[]{:S(2)}, u32[]{:S(2)}) %all-to-all-start.8) | async-done | bytes 327712 | tf_op jit(solution)/shard_map/all_to_all | solution.py:99
  172.0 8.5 %all-to-all-start.4 = ((bf16[256,8,128]{2,0,1:T(8,128)(2,1)}), bf16[256,8,128]{2,0,1:T(8,128)(2,1)S(1)}, u32[]{:S(2)}, u32[]{:S(2)}) async-start(bf16[256,8,128]{2,0,1:T(8,128)(2,1)} %bitcast.54), calls=%async_computation.4 | async-start | bytes 1048576 | tf_op jit(solution)/shard_map/all_to_all | solution.py:165
  180.5 9.4 %all-to-all-done.4 = bf16[256,8,128]{2,0,1:T(8,128)(2,1)S(1)} async-done(((bf16[256,8,128]{2,0,1:T(8,128)(2,1)}), bf16[256,8,128]{2,0,1:T(8,128)(2,1)S(1)}, u32[]{:S(2)}, u32[]{:S(2)}) %all-to-all-start.4) | async-done | bytes 524320 | tf_op jit(solution)/shard_map/all_to_all | solution.py:165
  190.9 5.3 %all-to-all-start.9 = ((f32[32,5,512]{2,1,0:T(8,128)}), f32[32,5,512]{2,1,0:T(8,128)S(1)}, u32[]{:S(2)}, u32[]{:S(2)}) async-start(f32[32,5,512]{2,1,0:T(8,128)} %broadcast_in_dim.9), calls=%async_computation.9 | async-start | bytes 1048576 | tf_op jit(solution)/shard_map/all_to_all | solution.py:100
  198.6 11.7 %all-to-all-done.9 = f32[32,5,512]{2,1,0:T(8,128)S(1)} async-done(((f32[32,5,512]{2,1,0:T(8,128)}), f32[32,5,512]{2,1,0:T(8,128)S(1)}, u32[]{:S(2)}, u32[]{:S(2)}) %all-to-all-start.9) | async-done | bytes 327712 | tf_op jit(solution)/shard_map/all_to_all | solution.py:100
  211.0 7.8 %all-to-all-start.5 = ((bf16[32,2,128,128]{3,2,1,0:T(8,128)(2,1)}), bf16[32,2,128,128]{3,2,1,0:T(8,128)(2,1)S(1)}, u32[]{:S(2)}, u32[]{:S(2)}) async-start(bf16[32,2,128,128]{3,2,1,0:T(8,128)(2,1)} %bitcast.62), calls=%async_computation.5 | async-start | bytes 4194304 | tf_op jit(solution)/shard_map/all_to_all | solution.py:168
  220.6 47.5 %all-to-all-done.5 = bf16[32,2,128,128]{3,2,1,0:T(8,128)(2,1)S(1)} async-done(((bf16[32,2,128,128]{3,2,1,0:T(8,128)(2,1)}), bf16[32,2,128,128]{3,2,1,0:T(8,128)(2,1)S(1)}, u32[]{:S(2)}, u32[]{:S(2)}) %all-to-all-start.5) | async-done | bytes 2097184 | tf_op jit(solution)/shard_map/all_to_all | solution.py:168
  270.9 5.5 %all-to-all-start.10 = ((f32[8,129,512]{2,1,0:T(8,128)}), f32[8,129,512]{2,1,0:T(8,128)S(1)}, u32[]{:S(2)}, u32[]{:S(2)}) async-start(f32[8,129,512]{2,1,0:T(8,128)} %broadcast_in_dim.10), calls=%async_computation.10 | async-start | bytes 4456448 | tf_op jit(solution)/shard_map/all_to_all | solution.py:103
  282.5 7.1 %shard_map.140.acc_in = f32[16,128,128]{2,1,0:T(8,128)} custom-call(s32[16,16]{1,0:T(8,128)} %bitcast.73, s32[16,16]{1,0:T(8,128)} %bitcast.75, bf16[16,128,128]{2,1,0:T(8,128)(2,1)} %bitcast.65, bf16[16,128,128]{2,1,0:T(8,128)(2,1)} %bitcast.56), custom_call_target="tpu_custom_call" | custom-call | flops 1073741824 | bytes 2097152 | tf_op jit(solution)/shard_map/pallas_call | solution.py:69
  289.5 11.6 %shard_map.141 = bf16[16,128,128]{2,1,0:T(8,128)(2,1)} custom-call(s32[64]{0:T(128)} %reshape.132.dest, s32[64]{0:T(128)} %reshape.133.banks, s32[64]{0:T(128)} %reshape.141.live, bf16[16,128,128]{2,1,0:T(8,128)(2,1)} %bitcast.66, f32[16,128,128]{2,1,0:T(8,128)} %shard_map.140.acc_in, bf16[64,128,128]{2,1,0:T(8,128)(2,1)} %bitcast.59), custom_call_target="tpu_custom_call" | custom-call | flops 268435456 | bytes 4194304 | tf_op jit(solution)/shard_map/pallas_call | solution.py:80
  304.2 4.9 %all-to-all-start.6 = ((bf16[8,256,128]{2,1,0:T(8,128)(2,1)}), bf16[8,256,128]{2,1,0:T(8,128)(2,1)}, u32[]{:S(2)}, u32[]{:S(2)}) async-start(bf16[8,256,128]{2,1,0:T(8,128)(2,1)} %bitcast.67), calls=%async_computation.6 | async-start | bytes 1048576 | tf_op jit(solution)/shard_map/all_to_all | solution.py:181
  315.2 3.5 %all-to-all-done.6 = bf16[8,256,128]{2,1,0:T(8,128)(2,1)} async-done(((bf16[8,256,128]{2,1,0:T(8,128)(2,1)}), bf16[8,256,128]{2,1,0:T(8,128)(2,1)}, u32[]{:S(2)}, u32[]{:S(2)}) %all-to-all-start.6) | async-done | bytes 524320 | tf_op jit(solution)/shard_map/all_to_all | solution.py:181
  (77 shorter events, 47.8 us)
Async XLA Ops:
  0.6 104.5 %copy-start = (bf16[1024,512]{1,0:T(8,128)(2,1)S(1)}, bf16[1024,512]{1,0:T(8,128)(2,1)}, u32[]{:S(2)}) copy-start(bf16[1024,512]{1,0:T(8,128)(2,1)} %param.12) | copy-start | bytes 3145732
  0.6 8.7 %copy-start.8 = (s32[1,4]{1,0:T(1,128)S(1)}, s32[1,4]{1,0:T(1,128)}, u32[]{:S(2)}) copy-start(s32[1,4]{1,0:T(1,128)} %param.18) | copy-start | bytes 52
  0.7 9.3 %copy-start.7 = (s32[32,32,2]{1,2,0:T(2,128)S(1)}, s32[32,32,2]{1,2,0:T(2,128)}, u32[]{:S(2)}) copy-start(s32[32,32,2]{1,2,0:T(2,128)} %param.19) | copy-start | bytes 24580
  2.7 16.1 %all-to-all-start = ((bf16[256,8,128]{2,0,1:T(8,128)(2,1)}), bf16[256,8,128]{2,0,1:T(8,128)(2,1)S(1)}, u32[]{:S(2)}, u32[]{:S(2)}) async-start(bf16[256,8,128]{2,0,1:T(8,128)(2,1)} %copy_bitcast_fusion.2), calls=%async_computation | async-start | bytes 1048576 | tf_op jit(solution)/shard_map/all_to_all | solution.py:128
  18.8 2.1 copy-start.2
  21.0 10.5 %copy-start.10 = (s32[1,32,2]{1,2,0:T(2,128)S(1)}, s32[1,32,2]{1,2,0:T(2,128)}, u32[]{:S(2)}) copy-start(s32[1,32,2]{1,2,0:T(2,128)} %param.20) | copy-start | bytes 772
  21.0 11.2 %copy-start.9 = (s32[1,32,2]{1,2,0:T(2,128)S(1)}, s32[1,32,2]{1,2,0:T(2,128)}, u32[]{:S(2)}) copy-start(s32[1,32,2]{1,2,0:T(2,128)} %param.21) | copy-start | bytes 772
  21.0 59.2 %all-to-all-start.1 = ((bf16[32,2,128,128]{3,2,1,0:T(8,128)(2,1)}), bf16[32,2,128,128]{3,2,1,0:T(8,128)(2,1)S(1)}, u32[]{:S(2)}, u32[]{:S(2)}) async-start(bf16[32,2,128,128]{3,2,1,0:T(8,128)(2,1)} %bitcast.61), calls=%async_computation.1 | async-start | bytes 4194304 | tf_op jit(solution)/shard_map/all_to_all | solution.py:139
  80.2 1.3 copy-start.4
  89.8 15.3 %copy-start.13 = (f32[512]{0:T(512)S(1)}, f32[512]{0:T(512)}, u32[]{:S(2)}) copy-start(f32[512]{0:T(512)} %param.13) | copy-start | bytes 6148
  89.8 16.5 %copy-start.6 = (bf16[256,512]{1,0:T(8,128)(2,1)S(1)}, bf16[256,512]{1,0:T(8,128)(2,1)}, u32[]{:S(2)}) copy-start(bf16[256,512]{1,0:T(8,128)(2,1)} %param.14) | copy-start | bytes 786436
  108.7 32.3 %all-to-all-start.7 = ((f32[8,129,512]{2,1,0:T(8,128)}), f32[8,129,512]{2,1,0:T(8,128)S(1)}, u32[]{:S(2)}, u32[]{:S(2)}) async-start(f32[8,129,512]{2,1,0:T(8,128)} %reshape.136), calls=%async_computation.7 | async-start | bytes 4456448 | tf_op jit(solution)/shard_map/all_to_all | solution.py:96
  141.0 14.3 %all-to-all-start.3 = ((s32[32,1,2]{2,1,0:T(1,128)}), s32[32,1,2]{2,1,0:T(1,128)S(1)}, u32[]{:S(2)}, u32[]{:S(2)}) async-start(s32[32,1,2]{2,1,0:T(1,128)} %copy.44), calls=%async_computation.3 | async-start | bytes 32768 | tf_op jit(solution)/shard_map/all_to_all | solution.py:169
  155.3 16.7 %all-to-all-start.8 = ((f32[32,5,512]{2,1,0:T(8,128)}), f32[32,5,512]{2,1,0:T(8,128)S(1)}, u32[]{:S(2)}, u32[]{:S(2)}) async-start(f32[32,5,512]{2,1,0:T(8,128)} %reshape.137), calls=%async_computation.8 | async-start | bytes 1048576 | tf_op jit(solution)/shard_map/all_to_all | solution.py:99
  159.7 36.5 %copy-start.11 = (s32[1,32,2]{1,2,0:T(2,128)S(1)}, s32[1,32,2]{1,2,0:T(2,128)}, u32[]{:S(2)}) copy-start(s32[1,32,2]{1,2,0:T(2,128)} %param.20) | copy-start | bytes 772
  172.0 18.0 %all-to-all-start.4 = ((bf16[256,8,128]{2,0,1:T(8,128)(2,1)}), bf16[256,8,128]{2,0,1:T(8,128)(2,1)S(1)}, u32[]{:S(2)}, u32[]{:S(2)}) async-start(bf16[256,8,128]{2,0,1:T(8,128)(2,1)} %bitcast.54), calls=%async_computation.4 | async-start | bytes 1048576 | tf_op jit(solution)/shard_map/all_to_all | solution.py:165
  190.0 8.6 %copy-start.1 = (bf16[256,8,128]{2,0,1:T(8,128)(2,1)}, bf16[256,8,128]{2,0,1:T(8,128)(2,1)S(1)}, u32[]{:S(2)}) copy-start(bf16[256,8,128]{2,0,1:T(8,128)(2,1)S(1)} %all-to-all-done.4) | copy-start | bytes 1572868
  190.9 19.3 %all-to-all-start.9 = ((f32[32,5,512]{2,1,0:T(8,128)}), f32[32,5,512]{2,1,0:T(8,128)S(1)}, u32[]{:S(2)}, u32[]{:S(2)}) async-start(f32[32,5,512]{2,1,0:T(8,128)} %broadcast_in_dim.9), calls=%async_computation.9 | async-start | bytes 1048576 | tf_op jit(solution)/shard_map/all_to_all | solution.py:100
  210.2 0.8 copy-start.5
  211.0 57.1 %all-to-all-start.5 = ((bf16[32,2,128,128]{3,2,1,0:T(8,128)(2,1)}), bf16[32,2,128,128]{3,2,1,0:T(8,128)(2,1)S(1)}, u32[]{:S(2)}, u32[]{:S(2)}) async-start(bf16[32,2,128,128]{3,2,1,0:T(8,128)(2,1)} %bitcast.62), calls=%async_computation.5 | async-start | bytes 4194304 | tf_op jit(solution)/shard_map/all_to_all | solution.py:168
  268.1 2.8 copy-start.3
  270.9 7.6 %copy-start.12 = (s32[1,32,2]{1,2,0:T(2,128)S(1)}, s32[1,32,2]{1,2,0:T(2,128)}, u32[]{:S(2)}) copy-start(s32[1,32,2]{1,2,0:T(2,128)} %get-tuple-element.7) | copy-start | bytes 772
  270.9 33.3 %all-to-all-start.10 = ((f32[8,129,512]{2,1,0:T(8,128)}), f32[8,129,512]{2,1,0:T(8,128)S(1)}, u32[]{:S(2)}, u32[]{:S(2)}) async-start(f32[8,129,512]{2,1,0:T(8,128)} %broadcast_in_dim.10), calls=%async_computation.10 | async-start | bytes 4456448 | tf_op jit(solution)/shard_map/all_to_all | solution.py:103
  304.2 14.5 %all-to-all-start.6 = ((bf16[8,256,128]{2,1,0:T(8,128)(2,1)}), bf16[8,256,128]{2,1,0:T(8,128)(2,1)}, u32[]{:S(2)}, u32[]{:S(2)}) async-start(bf16[8,256,128]{2,1,0:T(8,128)(2,1)} %bitcast.67), calls=%async_computation.6 | async-start | bytes 1048576 | tf_op jit(solution)/shard_map/all_to_all | solution.py:181

commit v2 on v1

--- a/solution.py
+++ b/solution.py
@@ -87,22 +87,15 @@
     )(dest, banks, live, bank, acc, blocks)
 
 
-def _all_reduce(x):
-    groups = lax.axis_size("grp")
+def _dom_sum(x):
     domains = lax.axis_size("dom")
     rows, width = x.shape
-    chunk = -(-rows // groups)
-    x = jnp.pad(x, ((0, chunk * groups - rows), (0, 0)))
-    y = lax.all_to_all(x.reshape(groups, chunk, width), "grp", 0, 0, tiled=True).sum(0)
-    piece = -(-chunk // domains)
-    y = jnp.pad(y, ((0, piece * domains - chunk), (0, 0)))
+    piece = -(-rows // domains)
+    y = jnp.pad(x, ((0, piece * domains - rows), (0, 0)))
     z = lax.all_to_all(y.reshape(domains, piece, width), "dom", 0, 0, tiled=True).sum(0)
     z = lax.all_to_all(
         jnp.broadcast_to(z[None], (domains, piece, width)), "dom", 0, 0, tiled=True
-    ).reshape(domains * piece, width)[:chunk]
-    z = lax.all_to_all(
-        jnp.broadcast_to(z[None], (groups, chunk, width)), "grp", 0, 0, tiled=True
-    ).reshape(groups * chunk, width)
+    ).reshape(domains * piece, width)
     return z[:rows]
 
 
@@ -155,18 +148,23 @@
     pre_act = jnp.dot(aggregated, weight, preferred_element_type=jnp.float32) + bias
     activations = jnp.maximum(pre_act, 0.0).astype(jnp.bfloat16)
     grad_pre = jnp.where(pre_act > 0, cotangent.astype(jnp.float32), 0.0).astype(jnp.bfloat16)
+    grad_full = lax.all_to_all(
+        jnp.broadcast_to(grad_pre[None], (groups,) + grad_pre.shape), "grp", 0, 0, tiled=True
+    ).reshape(part_rows, grad_pre.shape[1])
+    group_index = lax.axis_index("grp")
+    weight_rows = lax.dynamic_slice_in_dim(weight, group_index * narrow, narrow, 0)
+    grad_narrow = lax.dot_general(
+        grad_full, weight_rows, (((1,), (1,)), ((), ())), preferred_element_type=jnp.float32
+    ).astype(jnp.bfloat16)
+    grad_blocks = grad_narrow.reshape(blocks, tile_size, narrow)
     weight_part = lax.dot_general(
-        aggregated, grad_pre, (((0,), (0,)), ((), ())), preferred_element_type=jnp.float32
-    )
-    bias_part = jnp.sum(grad_pre.astype(jnp.float32), axis=0)
-    grad_agg = lax.dot_general(
-        grad_pre, weight, (((1,), (1,)), ((), ())), preferred_element_type=jnp.float32
-    ).astype(jnp.bfloat16)
-    grad_narrow = lax.all_to_all(grad_agg, "grp", split_axis=1, concat_axis=0, tiled=True)
-    grad_blocks = grad_narrow.reshape(blocks, tile_size, narrow)
+        agg_narrow, grad_full, (((0,), (0,)), ((), ())), preferred_element_type=jnp.float32
+    )
+    bias_part = jnp.sum(grad_full.astype(jnp.float32), axis=0)
 
     back_in = lax.all_to_all(grad_blocks[rows_in], "dom", 0, 0, tiled=True)
-    banks_back = lax.all_to_all(halo_banks[0], "dom", 0, 0, tiled=True)
+    all_banks = lax.all_gather(halo_banks[0], "dom", axis=0, tiled=False)
+    banks_back = lax.dynamic_index_in_dim(all_banks, domain_index, 1, keepdims=False)
     live_out = (outgoing >= 0).astype(jnp.int32).reshape(-1)
 
     local_back = _local(_bwd_local_kernel, cols_here, banks_here, bank_t, grad_blocks)
@@ -186,13 +184,19 @@
         tiled=True,
     )
     norm_scale = float(rows_here * groups * domains) ** (-0.5)
-    hidden = weight_part.shape[0]
-    summed = _all_reduce(jnp.concatenate([weight_part, bias_part[None]], axis=0))
+    summed = _dom_sum(jnp.concatenate([weight_part, bias_part[None]], axis=0))
+    weight_total = lax.all_to_all(
+        jnp.broadcast_to(summed[None, :narrow], (groups, narrow, summed.shape[1])),
+        "grp",
+        0,
+        0,
+        tiled=True,
+    ).reshape(groups * narrow, summed.shape[1])
     return (
         activations,
         grad_nodes,
-        summed[:hidden] * norm_scale,
-        summed[hidden] * norm_scale,
+        weight_total * norm_scale,
+        summed[narrow] * norm_scale,
     )
 
 

time: 322 us -> 330 us (1.025)
  blocking collectives: 14 us -> 98.1 us
  waiting for transfers between devices: 164 us -> 107 us
  starting transfers between devices: 63.2 us -> 51.5 us
  local copies, waits for them, and re-layouts: 31.7 us -> 25.1 us
    all_to_all x6 -> x2, waiting for transfers between devices: 68.6 us -> 8.79 us  [the longest x1 8.78 us: _dom_sum(): lax.all_to_all(jnp.broadcast_to(z[None], (domains, piece, width)), 'dom',...]
    all_to_all x0 -> x2, blocking collectives: none -> 50.1 us  [the longest x1 30.1 us: per_device(): lax.all_to_all(jnp.broadcast_to(grad_pre[None], (groups,) + grad_pre.shap...]
    all_gather x0 -> x1, blocking collectives: none -> 33.9 us  [per_device(): all_banks = lax.all_gather(halo_banks[0], 'dom', axis=0, tiled=False)]
    all_to_all x6 -> x2, starting transfers between devices: 33.4 us -> 14.2 us  [the longest x1 8.1 us: _dom_sum(): lax.all_to_all(jnp.broadcast_to(z[None], (domains, piece, width)), 'dom',...]
    all_to_all x1, starting transfers between devices: 4.9 us -> 12.2 us  [per_device(): lax.all_to_all(grad_total.reshape(part_rows, narrow), 'grp', split_axis=0...]
    reshape x4 -> x2, local copies, waits for them, and re-layouts: 5.28 us -> 1.95 us  [the longest x1 1.1 us: _dom_sum(): z = lax.all_to_all(jnp.broadcast_to(z[None], (domains, piece, width)), 'd...]
  transfers between devices with their start and end apart: 10 -> 6, of which waited for: 10 -> 5; matrix products, arithmetic and copies ran while one was open for 9% -> 7% of each run, Pallas kernels for 8% -> 8%
where the time goes in v2:
time: 330 us; the launch traced here: 328 us
  waiting for transfers between devices  107 us (32%)
  blocking collectives  98.1 us (30%)
  starting transfers between devices  51.5 us (16%)
  Pallas kernels  34 us (10%)
  local copies, waits for them, and re-layouts  25.1 us (8%)
  other arithmetic  8.65 us (3%)
    all_to_all x1, waiting for transfers between devices, per_device(): back_in = lax.all_to_all(grad_blocks[rows_in], 'dom', 0, 0, tiled=True)  47.6 us
    all_to_all x1, waiting for transfers between devices, per_device(): remote = lax.all_to_all(feat_blocks[send_ids], 'dom', 0, 0, tiled=True)  39 us
    all_gather x1, blocking collectives, per_device(): all_banks = lax.all_gather(halo_banks[0], 'dom', axis=0, tiled=False)  33.9 us
    all_to_all x1, blocking collectives, per_device(): lax.all_to_all(jnp.broadcast_to(grad_pre[None], (groups,) + grad_pre.shap...  30.1 us
    pallas_call x2, Pallas kernels, _halo(): pl.pallas_call(_halo_kernel, out_shape=jax.ShapeDtypeStruct((n, tile, wid...  20.1 us
    all_to_all x1, blocking collectives, _dom_sum(): lax.all_to_all(y.reshape(domains, piece, width), 'dom', 0, 0, tiled=True)  20.1 us
    all_to_all x1, blocking collectives, per_device(): lax.all_to_all(agg_narrow, 'grp', split_axis=0, concat_axis=1, tiled=True)  14 us
    pallas_call x2, Pallas kernels, _local(): pl.pallas_call(kernel, out_shape=jax.ShapeDtypeStruct((n, tile, width), j...  14 us
  transfers between devices with their start and end apart: 6, of which 5 were waited for; matrix products, arithmetic and copies ran while one was open for 7% of the time, Pallas kernels for 8%

profile of v2, /device:TPU:1, one launch (start us, length us, event | category | flops | bytes accessed | tf_op | source)
XLA Modules:
  0.0 328.4 jit_solution(10024708023753974817)
XLA Ops:
  2.7 6.6 %all-to-all-start = ((bf16[256,8,128]{2,0,1:T(8,128)(2,1)}), bf16[256,8,128]{2,0,1:T(8,128)(2,1)S(1)}, u32[]{:S(2)}, u32[]{:S(2)}) async-start(bf16[256,8,128]{2,0,1:T(8,128)(2,1)} %copy_bitcast_fusion.1), calls=%async_computation | async-start | bytes 1048576 | tf_op jit(solution)/shard_map/all_to_all | solution.py:121
  9.9 2.6 compare_select_fusion.1
  12.7 6.1 %all-to-all-done = bf16[256,8,128]{2,0,1:T(8,128)(2,1)S(1)} async-done(((bf16[256,8,128]{2,0,1:T(8,128)(2,1)}), bf16[256,8,128]{2,0,1:T(8,128)(2,1)S(1)}, u32[]{:S(2)}, u32[]{:S(2)}) %all-to-all-start) | async-done | bytes 524320 | tf_op jit(solution)/shard_map/all_to_all | solution.py:121
  18.8 2.1 gather_fusion
  21.0 10.5 %all-to-all-start.1 = ((bf16[32,2,128,128]{3,2,1,0:T(8,128)(2,1)}), bf16[32,2,128,128]{3,2,1,0:T(8,128)(2,1)S(1)}, u32[]{:S(2)}, u32[]{:S(2)}) async-start(bf16[32,2,128,128]{3,2,1,0:T(8,128)(2,1)} %bitcast.57), calls=%async_computation.1 | async-start | bytes 4194304 | tf_op jit(solution)/shard_map/all_to_all | solution.py:132
  34.3 6.9 %shard_map.138.acc_in = f32[16,128,128]{2,1,0:T(8,128)} custom-call(s32[16,16]{1,0:T(8,128)} %bitcast.68, s32[16,16]{1,0:T(8,128)} %bitcast.70, bf16[16,128,128]{2,1,0:T(8,128)(2,1)} %bank_ref.3, bf16[16,128,128]{2,1,0:T(8,128)(2,1)} %bitcast.52), custom_call_target="tpu_custom_call" | custom-call | flops 1073741824 | bytes 2097152 | tf_op jit(solution)/shard_map/pallas_call | solution.py:69
  41.2 39.0 %all-to-all-done.1 = bf16[32,2,128,128]{3,2,1,0:T(8,128)(2,1)S(1)} async-done(((bf16[32,2,128,128]{3,2,1,0:T(8,128)(2,1)}), bf16[32,2,128,128]{3,2,1,0:T(8,128)(2,1)S(1)}, u32[]{:S(2)}, u32[]{:S(2)}) %all-to-all-start.1) | async-done | bytes 2097184 | tf_op jit(solution)/shard_map/all_to_all | solution.py:132
  81.5 8.4 %shard_map.139 = bf16[16,128,128]{2,1,0:T(8,128)(2,1)} custom-call(s32[64]{0:T(128)} %reshape_squeeze.6.dest, s32[64]{0:T(128)} %reshape_squeeze.7.banks, s32[64]{0:T(128)} %reshape.136.live, bf16[16,128,128]{2,1,0:T(8,128)(2,1)} %bank_ref.3, f32[16,128,128]{2,1,0:T(8,128)} %shard_map.138.acc_in, bf16[64,128,128]{2,1,0:T(8,128)(2,1)} %bitcast.56), custom_call_target="tpu_custom_call" | custom-call | flops 268435456 | bytes 4194304 | tf_op jit(solution)/shard_map/pallas_call | solution.py:80
  91.2 14.0 %all_to_all.84 = bf16[8,256,128]{1,2,0:T(8,128)(2,1)S(1)} all-to-all(bf16[8,256,128]{1,2,0:T(8,128)(2,1)S(1)} %copy.48), channel_id=1, replica_groups=mesh['dom'=32,'grp'=8] {'grp'}, dimensions={0} | all-to-all | bytes 1048576 | tf_op jit(solution)/shard_map/all_to_all | solution.py:147
  106.7 30.1 %all_to_all.85 = bf16[8,256,512]{2,1,0:T(8,128)(2,1)S(1)} all-to-all(bf16[8,256,512]{2,1,0:T(8,128)(2,1)S(1)} %broadcast_in_dim.10), channel_id=1, replica_groups=mesh['dom'=32,'grp'=8] {'grp'}, dimensions={0} | all-to-all | bytes 4194304 | tf_op jit(solution)/shard_map/all_to_all | solution.py:151
  138.5 20.1 %all_to_all.86 = f32[32,5,512]{2,1,0:T(8,128)} all-to-all(f32[32,5,512]{2,1,0:T(8,128)} %reshape.134), channel_id=1, replica_groups=mesh['dom'=32,'grp'=8] {'dom'}, dimensions={0} | all-to-all | bytes 655360 | tf_op jit(solution)/shard_map/all_to_all | solution.py:95
  160.5 8.1 %all-to-all-start.7 = ((f32[32,5,512]{2,1,0:T(8,128)}), f32[32,5,512]{2,1,0:T(8,128)}, u32[]{:S(2)}, u32[]{:S(2)}) async-start(f32[32,5,512]{2,1,0:T(8,128)} %broadcast_in_dim.12), calls=%async_computation.7 | async-start | bytes 1048576 | tf_op jit(solution)/shard_map/all_to_all | solution.py:96
  170.4 3.2 gather_fusion.1
  173.6 8.8 %all-to-all-done.7 = f32[32,5,512]{2,1,0:T(8,128)} async-done(((f32[32,5,512]{2,1,0:T(8,128)}), f32[32,5,512]{2,1,0:T(8,128)}, u32[]{:S(2)}, u32[]{:S(2)}) %all-to-all-start.7) | async-done | bytes 327712 | tf_op jit(solution)/shard_map/all_to_all | solution.py:96
  182.4 8.0 %all-to-all-start.4 = ((bf16[32,2,128,128]{3,2,1,0:T(8,128)(2,1)}), bf16[32,2,128,128]{3,2,1,0:T(8,128)(2,1)S(1)}, u32[]{:S(2)}, u32[]{:S(2)}) async-start(bf16[32,2,128,128]{3,2,1,0:T(8,128)(2,1)} %bitcast.58), calls=%async_computation.4 | async-start | bytes 4194304 | tf_op jit(solution)/shard_map/all_to_all | solution.py:165
  192.2 47.6 %all-to-all-done.4 = bf16[32,2,128,128]{3,2,1,0:T(8,128)(2,1)S(1)} async-done(((bf16[32,2,128,128]{3,2,1,0:T(8,128)(2,1)}), bf16[32,2,128,128]{3,2,1,0:T(8,128)(2,1)S(1)}, u32[]{:S(2)}, u32[]{:S(2)}) %all-to-all-start.4) | async-done | bytes 2097184 | tf_op jit(solution)/shard_map/all_to_all | solution.py:165
  239.8 2.7 broadcast_in_dim.13
  242.5 6.1 %all-to-all-start.8 = ((f32[8,128,512]{2,1,0:T(8,128)}), f32[8,128,512]{2,1,0:T(8,128)}, u32[]{:S(2)}, u32[]{:S(2)}) async-start(f32[8,128,512]{2,1,0:T(8,128)} %broadcast_in_dim.13), calls=%async_computation.8 | async-start | bytes 4194304 | tf_op jit(solution)/shard_map/all_to_all | solution.py:188
  252.0 33.9 %all_gather.3 = s32[32,32,2]{1,2,0:T(2,128)S(1)} all-gather(s32[1,32,2]{1,2,0:T(2,128)S(1)} %copy-done.9), channel_id=1, replica_groups=mesh['dom'=32,'grp'=8] {'dom'}, dimensions={0}, use_global_device_ids=true | all-gather | bytes 8448 | tf_op jit(solution)/shard_map/all_gather | solution.py:166
  287.2 7.0 %shard_map.140.acc_in = f32[16,128,128]{2,1,0:T(8,128)} custom-call(s32[16,16]{1,0:T(8,128)} %bitcast.69, s32[16,16]{1,0:T(8,128)} %bitcast.71, bf16[16,128,128]{2,1,0:T(8,128)(2,1)} %bitcast.61, bf16[16,128,128]{2,1,0:T(8,128)(2,1)} %bitcast.54), custom_call_target="tpu_custom_call" | custom-call | flops 1073741824 | bytes 2097152 | tf_op jit(solution)/shard_map/pallas_call | solution.py:69
  294.3 11.6 %shard_map.141 = bf16[16,128,128]{2,1,0:T(8,128)(2,1)} custom-call(s32[64]{0:T(128)} %reshape.128.dest, s32[64]{0:T(128)} %reshape.129.banks, s32[64]{0:T(128)} %reshape.137.live, bf16[16,128,128]{2,1,0:T(8,128)(2,1)} %bitcast.62, f32[16,128,128]{2,1,0:T(8,128)} %shard_map.140.acc_in, bf16[64,128,128]{2,1,0:T(8,128)(2,1)} %bitcast.55), custom_call_target="tpu_custom_call" | custom-call | flops 268435456 | bytes 4194304 | tf_op jit(solution)/shard_map/pallas_call | solution.py:80
  305.9 12.2 %all-to-all-start.5 = ((bf16[8,256,128]{2,1,0:T(8,128)(2,1)}), bf16[8,256,128]{2,1,0:T(8,128)(2,1)S(1)}, u32[]{:S(2)}, u32[]{:S(2)}) async-start(bf16[8,256,128]{2,1,0:T(8,128)(2,1)} %bitcast.63), calls=%async_computation.5 | async-start | bytes 1048576 | tf_op jit(solution)/shard_map/all_to_all | solution.py:179
  318.7 3.2 broadcast_multiply_fusion
  321.9 5.7 %all-to-all-done.5 = bf16[8,256,128]{2,1,0:T(8,128)(2,1)S(1)} async-done(((bf16[8,256,128]{2,1,0:T(8,128)(2,1)}), bf16[8,256,128]{2,1,0:T(8,128)(2,1)S(1)}, u32[]{:S(2)}, u32[]{:S(2)}) %all-to-all-start.5) | async-done | bytes 524320 | tf_op jit(solution)/shard_map/all_to_all | solution.py:179
  (60 shorter events, 23.2 us)
Async XLA Ops:
  0.6 104.6 %copy-start = (bf16[1024,512]{1,0:T(8,128)(2,1)S(1)}, bf16[1024,512]{1,0:T(8,128)(2,1)}, u32[]{:S(2)}) copy-start(bf16[1024,512]{1,0:T(8,128)(2,1)} %param.12) | copy-start | bytes 3145732
  0.6 8.7 %copy-start.7 = (s32[1,4]{1,0:T(1,128)S(1)}, s32[1,4]{1,0:T(1,128)}, u32[]{:S(2)}) copy-start(s32[1,4]{1,0:T(1,128)} %param.18) | copy-start | bytes 52
  0.7 9.3 %copy-start.6 = (s32[32,32,2]{1,2,0:T(2,128)S(1)}, s32[32,32,2]{1,2,0:T(2,128)}, u32[]{:S(2)}) copy-start(s32[32,32,2]{1,2,0:T(2,128)} %param.19) | copy-start | bytes 24580
  0.7 9.3 %copy-start.8 = (s32[1,32,2]{1,2,0:T(2,128)S(1)}, s32[1,32,2]{1,2,0:T(2,128)}, u32[]{:S(2)}) copy-start(s32[1,32,2]{1,2,0:T(2,128)} %param.20) | copy-start | bytes 772
  2.7 16.1 %all-to-all-start = ((bf16[256,8,128]{2,0,1:T(8,128)(2,1)}), bf16[256,8,128]{2,0,1:T(8,128)(2,1)S(1)}, u32[]{:S(2)}, u32[]{:S(2)}) async-start(bf16[256,8,128]{2,0,1:T(8,128)(2,1)} %copy_bitcast_fusion.1), calls=%async_computation | async-start | bytes 1048576 | tf_op jit(solution)/shard_map/all_to_all | solution.py:121
  18.8 2.1 copy-start.1
  21.0 11.2 %copy-start.9 = (s32[1,32,2]{1,2,0:T(2,128)S(1)}, s32[1,32,2]{1,2,0:T(2,128)}, u32[]{:S(2)}) copy-start(s32[1,32,2]{1,2,0:T(2,128)} %param.21) | copy-start | bytes 772
  21.0 59.2 %all-to-all-start.1 = ((bf16[32,2,128,128]{3,2,1,0:T(8,128)(2,1)}), bf16[32,2,128,128]{3,2,1,0:T(8,128)(2,1)S(1)}, u32[]{:S(2)}, u32[]{:S(2)}) async-start(bf16[32,2,128,128]{3,2,1,0:T(8,128)(2,1)} %bitcast.57), calls=%async_computation.1 | async-start | bytes 4194304 | tf_op jit(solution)/shard_map/all_to_all | solution.py:132
  80.2 1.3 copy-start.3
  89.9 15.3 %copy-start.10 = (f32[512]{0:T(512)S(1)}, f32[512]{0:T(512)}, u32[]{:S(2)}) copy-start(f32[512]{0:T(512)} %param.13) | copy-start | bytes 6148
  89.9 16.5 %copy-start.5 = (bf16[256,512]{1,0:T(8,128)(2,1)S(1)}, bf16[256,512]{1,0:T(8,128)(2,1)}, u32[]{:S(2)}) copy-start(bf16[256,512]{1,0:T(8,128)(2,1)} %param.14) | copy-start | bytes 786436
  106.7 30.1 %copy-start.4 = (bf16[16,128,128]{2,1,0:T(8,128)(2,1)S(1)}, bf16[16,128,128]{2,1,0:T(8,128)(2,1)}, u32[]{:S(2)}) copy-start(bf16[16,128,128]{2,1,0:T(8,128)(2,1)} %shard_map.139) | copy-start | bytes 1572868
  160.5 21.8 %all-to-all-start.7 = ((f32[32,5,512]{2,1,0:T(8,128)}), f32[32,5,512]{2,1,0:T(8,128)}, u32[]{:S(2)}, u32[]{:S(2)}) async-start(f32[32,5,512]{2,1,0:T(8,128)} %broadcast_in_dim.12), calls=%async_computation.7 | async-start | bytes 1048576 | tf_op jit(solution)/shard_map/all_to_all | solution.py:96
  182.4 57.4 %all-to-all-start.4 = ((bf16[32,2,128,128]{3,2,1,0:T(8,128)(2,1)}), bf16[32,2,128,128]{3,2,1,0:T(8,128)(2,1)S(1)}, u32[]{:S(2)}, u32[]{:S(2)}) async-start(bf16[32,2,128,128]{3,2,1,0:T(8,128)(2,1)} %bitcast.58), calls=%async_computation.4 | async-start | bytes 4194304 | tf_op jit(solution)/shard_map/all_to_all | solution.py:165
  239.8 2.7 copy-start.2
  242.5 63.4 %all-to-all-start.8 = ((f32[8,128,512]{2,1,0:T(8,128)}), f32[8,128,512]{2,1,0:T(8,128)}, u32[]{:S(2)}, u32[]{:S(2)}) async-start(f32[8,128,512]{2,1,0:T(8,128)} %broadcast_in_dim.13), calls=%async_computation.8 | async-start | bytes 4194304 | tf_op jit(solution)/shard_map/all_to_all | solution.py:188
  305.9 21.7 %all-to-all-start.5 = ((bf16[8,256,128]{2,1,0:T(8,128)(2,1)}), bf16[8,256,128]{2,1,0:T(8,128)(2,1)S(1)}, u32[]{:S(2)}, u32[]{:S(2)}) async-start(bf16[8,256,128]{2,1,0:T(8,128)(2,1)} %bitcast.63), calls=%async_computation.5 | async-start | bytes 1048576 | tf_op jit(solution)/shard_map/all_to_all | solution.py:179

commit v3 on v2

--- a/solution.py
+++ b/solution.py
@@ -55,7 +55,9 @@
         @pl.when(live[j] > 0)
         def _():
             acc_ref[dest[j]] += jnp.dot(
-                bank_ref[banks[j]], blocks_ref[j], preferred_element_type=jnp.float32
+                bank_ref[banks[j]],
+                blocks_ref[j, pl.ds(0, acc_ref.shape[1]), :],
+                preferred_element_type=jnp.float32,
             )
 
         return carry
@@ -162,9 +164,12 @@
     )
     bias_part = jnp.sum(grad_full.astype(jnp.float32), axis=0)
 
-    back_in = lax.all_to_all(grad_blocks[rows_in], "dom", 0, 0, tiled=True)
-    all_banks = lax.all_gather(halo_banks[0], "dom", axis=0, tiled=False)
-    banks_back = lax.dynamic_index_in_dim(all_banks, domain_index, 1, keepdims=False)
+    bank_rows = jnp.broadcast_to(
+        halo_banks[0].astype(jnp.bfloat16)[:, :, None, None], (domains, slot_count, 8, narrow)
+    )
+    payload = jnp.concatenate([grad_blocks[rows_in], bank_rows], axis=2)
+    back_in = lax.all_to_all(payload, "dom", 0, 0, tiled=True)
+    banks_back = back_in[:, :, tile_size, 0].astype(jnp.int32)
     live_out = (outgoing >= 0).astype(jnp.int32).reshape(-1)
 
     local_back = _local(_bwd_local_kernel, cols_here, banks_here, bank_t, grad_blocks)
@@ -174,7 +179,7 @@
         live_out,
         bank_t,
         local_back,
-        back_in.reshape(domains * slot_count, tile_size, narrow),
+        back_in.reshape(domains * slot_count, tile_size + 8, narrow),
     )
     grad_nodes = lax.all_to_all(
         grad_total.reshape(part_rows, narrow),

time: 330 us -> 293 us (0.89)
  blocking collectives: 98.1 us -> 64.5 us
  starting transfers between devices: 51.5 us -> 43.4 us
  other arithmetic: 8.65 us -> 12.8 us
    all_gather x1 -> x0, blocking collectives: 33.9 us -> none  [per_device(): all_banks = lax.all_gather(halo_banks[0], 'dom', axis=0, tiled=False)]
    all_to_all x1, starting transfers between devices: 12.2 us -> 4.27 us  [per_device(): lax.all_to_all(grad_total.reshape(part_rows, narrow), 'grp', split_axis=0...]
  transfers between devices with their start and end apart: 6 -> 6, of which waited for: 5 -> 6; matrix products, arithmetic and copies ran while one was open for 7% -> 9% of each run, Pallas kernels for 8% -> 9%
where the time goes in v3:
time: 293 us; the launch traced here: 292 us
  waiting for transfers between devices  109 us (37%)
  blocking collectives  64.5 us (22%)
  starting transfers between devices  43.4 us (15%)
  Pallas kernels  34 us (12%)
  local copies, waits for them, and re-layouts  23.6 us (8%)
  other arithmetic  12.8 us (4%)
  matrix products  3.13 us (1%)
    all_to_all x1, waiting for transfers between devices, per_device(): back_in = lax.all_to_all(payload, 'dom', 0, 0, tiled=True)  49.3 us
    all_to_all x1, waiting for transfers between devices, per_device(): remote = lax.all_to_all(feat_blocks[send_ids], 'dom', 0, 0, tiled=True)  39 us
    all_to_all x1, blocking collectives, per_device(): lax.all_to_all(jnp.broadcast_to(grad_pre[None], (groups,) + grad_pre.shap...  30.1 us
    all_to_all x1, blocking collectives, _dom_sum(): lax.all_to_all(y.reshape(domains, piece, width), 'dom', 0, 0, tiled=True)  20.4 us
    pallas_call x2, Pallas kernels, _halo(): pl.pallas_call(_halo_kernel, out_shape=jax.ShapeDtypeStruct((n, tile, wid...  20 us
    all_to_all x1, blocking collectives, per_device(): lax.all_to_all(agg_narrow, 'grp', split_axis=0, concat_axis=1, tiled=True)  14 us
    pallas_call x2, Pallas kernels, _local(): pl.pallas_call(kernel, out_shape=jax.ShapeDtypeStruct((n, tile, width), j...  14 us
    all_to_all x1, starting transfers between devices, per_device(): remote = lax.all_to_all(feat_blocks[send_ids], 'dom', 0, 0, tiled=True)  10.5 us
  transfers between devices with their start and end apart: 6, of which 6 were waited for; matrix products, arithmetic and copies ran while one was open for 9% of the time, Pallas kernels for 9%

profile of v3, /device:TPU:1, one launch (start us, length us, event | category | flops | bytes accessed | tf_op | source)
XLA Modules:
  0.0 291.6 jit_solution(10352277391112573860)
XLA Ops:
  0.7 2.0 copy_bitcast_fusion.1
  2.7 6.6 %all-to-all-start = ((bf16[256,8,128]{2,0,1:T(8,128)(2,1)}), bf16[256,8,128]{2,0,1:T(8,128)(2,1)S(1)}, u32[]{:S(2)}, u32[]{:S(2)}) async-start(bf16[256,8,128]{2,0,1:T(8,128)(2,1)} %copy_bitcast_fusion.1), calls=%async_computation | async-start | bytes 1048576 | tf_op jit(solution)/shard_map/all_to_all | solution.py:123
  9.9 2.6 compare_select_fusion.1
  12.7 6.1 %all-to-all-done = bf16[256,8,128]{2,0,1:T(8,128)(2,1)S(1)} async-done(((bf16[256,8,128]{2,0,1:T(8,128)(2,1)}), bf16[256,8,128]{2,0,1:T(8,128)(2,1)S(1)}, u32[]{:S(2)}, u32[]{:S(2)}) %all-to-all-start) | async-done | bytes 524320 | tf_op jit(solution)/shard_map/all_to_all | solution.py:123
  18.8 2.1 gather_fusion
  21.0 10.5 %all-to-all-start.1 = ((bf16[32,2,128,128]{3,2,1,0:T(8,128)(2,1)}), bf16[32,2,128,128]{3,2,1,0:T(8,128)(2,1)S(1)}, u32[]{:S(2)}, u32[]{:S(2)}) async-start(bf16[32,2,128,128]{3,2,1,0:T(8,128)(2,1)} %bitcast.59), calls=%async_computation.1 | async-start | bytes 4194304 | tf_op jit(solution)/shard_map/all_to_all | solution.py:134
  34.3 6.9 %shard_map.138.acc_in = f32[16,128,128]{2,1,0:T(8,128)} custom-call(s32[16,16]{1,0:T(8,128)} %bitcast.70, s32[16,16]{1,0:T(8,128)} %bitcast.72, bf16[16,128,128]{2,1,0:T(8,128)(2,1)} %bank_ref.3, bf16[16,128,128]{2,1,0:T(8,128)(2,1)} %bitcast.54), custom_call_target="tpu_custom_call" | custom-call | flops 1073741824 | bytes 2097152 | tf_op jit(solution)/shard_map/pallas_call | solution.py:71
  41.2 39.0 %all-to-all-done.1 = bf16[32,2,128,128]{3,2,1,0:T(8,128)(2,1)S(1)} async-done(((bf16[32,2,128,128]{3,2,1,0:T(8,128)(2,1)}), bf16[32,2,128,128]{3,2,1,0:T(8,128)(2,1)S(1)}, u32[]{:S(2)}, u32[]{:S(2)}) %all-to-all-start.1) | async-done | bytes 2097184 | tf_op jit(solution)/shard_map/all_to_all | solution.py:134
  81.5 8.4 %shard_map.139 = bf16[16,128,128]{2,1,0:T(8,128)(2,1)} custom-call(s32[64]{0:T(128)} %reshape_squeeze.6.dest, s32[64]{0:T(128)} %reshape_squeeze.7.banks, s32[64]{0:T(128)} %reshape.141.live, bf16[16,128,128]{2,1,0:T(8,128)(2,1)} %bank_ref.3, f32[16,128,128]{2,1,0:T(8,128)} %shard_map.138.acc_in, bf16[64,128,128]{2,1,0:T(8,128)(2,1)} %bitcast.58), custom_call_target="tpu_custom_call" | custom-call | flops 268435456 | bytes 4194304 | tf_op jit(solution)/shard_map/pallas_call | solution.py:82
  91.2 14.0 %all_to_all.84 = bf16[8,256,128]{1,2,0:T(8,128)(2,1)S(1)} all-to-all(bf16[8,256,128]{1,2,0:T(8,128)(2,1)S(1)} %copy.55), channel_id=1, replica_groups=mesh['dom'=32,'grp'=8] {'grp'}, dimensions={0} | all-to-all | bytes 1048576 | tf_op jit(solution)/shard_map/all_to_all | solution.py:149
  106.7 30.1 %all_to_all.85 = bf16[8,256,512]{2,1,0:T(8,128)(2,1)S(1)} all-to-all(bf16[8,256,512]{2,1,0:T(8,128)(2,1)S(1)} %broadcast_in_dim.12), channel_id=1, replica_groups=mesh['dom'=32,'grp'=8] {'grp'}, dimensions={0} | all-to-all | bytes 4194304 | tf_op jit(solution)/shard_map/all_to_all | solution.py:153
  138.5 20.4 %all_to_all.86 = f32[32,5,512]{2,1,0:T(8,128)} all-to-all(f32[32,5,512]{2,1,0:T(8,128)} %reshape.139), channel_id=1, replica_groups=mesh['dom'=32,'grp'=8] {'dom'}, dimensions={0} | all-to-all | bytes 655360 | tf_op jit(solution)/shard_map/all_to_all | solution.py:97
  160.8 8.1 %all-to-all-start.7 = ((f32[32,5,512]{2,1,0:T(8,128)}), f32[32,5,512]{2,1,0:T(8,128)}, u32[]{:S(2)}, u32[]{:S(2)}) async-start(f32[32,5,512]{2,1,0:T(8,128)} %broadcast_in_dim.15), calls=%async_computation.7 | async-start | bytes 1048576 | tf_op jit(solution)/shard_map/all_to_all | solution.py:98
  170.8 2.0 gather_fusion.1
  174.5 8.2 %all-to-all-done.7 = f32[32,5,512]{2,1,0:T(8,128)} async-done(((f32[32,5,512]{2,1,0:T(8,128)}), f32[32,5,512]{2,1,0:T(8,128)}, u32[]{:S(2)}, u32[]{:S(2)}) %all-to-all-start.7) | async-done | bytes 327712 | tf_op jit(solution)/shard_map/all_to_all | solution.py:98
  182.7 7.9 %all-to-all-start.4 = ((bf16[32,2,136,128]{3,2,1,0:T(8,128)(2,1)}), bf16[32,2,136,128]{3,2,1,0:T(8,128)(2,1)S(1)}, u32[]{:S(2)}, u32[]{:S(2)}) async-start(bf16[32,2,136,128]{3,2,1,0:T(8,128)(2,1)} %pad_maximum_fusion), calls=%async_computation.4 | async-start | bytes 4456448 | tf_op jit(solution)/shard_map/all_to_all | solution.py:171
  193.4 49.3 %all-to-all-done.4 = bf16[32,2,136,128]{3,2,1,0:T(8,128)(2,1)S(1)} async-done(((bf16[32,2,136,128]{3,2,1,0:T(8,128)(2,1)}), bf16[32,2,136,128]{3,2,1,0:T(8,128)(2,1)S(1)}, u32[]{:S(2)}, u32[]{:S(2)}) %all-to-all-start.4) | async-done | bytes 2228256 | tf_op jit(solution)/shard_map/all_to_all | solution.py:171
  244.5 6.0 %all-to-all-start.8 = ((f32[8,128,512]{2,1,0:T(8,128)}), f32[8,128,512]{2,1,0:T(8,128)}, u32[]{:S(2)}, u32[]{:S(2)}) async-start(f32[8,128,512]{2,1,0:T(8,128)} %broadcast_in_dim.16), calls=%async_computation.8 | async-start | bytes 4194304 | tf_op jit(solution)/shard_map/all_to_all | solution.py:193
  250.5 2.0 copy.60
  254.7 7.1 %shard_map.140.acc_in = f32[16,128,128]{2,1,0:T(8,128)} custom-call(s32[16,16]{1,0:T(8,128)} %bitcast.71, s32[16,16]{1,0:T(8,128)} %bitcast.73, bf16[16,128,128]{2,1,0:T(8,128)(2,1)} %bitcast.64, bf16[16,128,128]{2,1,0:T(8,128)(2,1)} %bitcast.56), custom_call_target="tpu_custom_call" | custom-call | flops 1073741824 | bytes 2097152 | tf_op jit(solution)/shard_map/pallas_call | solution.py:71
  263.6 11.6 %shard_map.141 = bf16[16,128,128]{2,1,0:T(8,128)(2,1)} custom-call(s32[64]{0:T(128)} %reshape.134.dest, s32[64]{0:T(128)} %reshape.142.banks, s32[64]{0:T(128)} %reshape.143.live, bf16[16,128,128]{2,1,0:T(8,128)(2,1)} %bitcast.65, f32[16,128,128]{2,1,0:T(8,128)} %shard_map.140.acc_in, bf16[64,136,128]{2,1,0:T(8,128)(2,1)} %bitcast.57), custom_call_target="tpu_custom_call" | custom-call | flops 268435456 | bytes 4325376 | tf_op jit(solution)/shard_map/pallas_call | solution.py:82
  276.9 4.3 %all-to-all-start.5 = ((bf16[8,256,128]{2,1,0:T(8,128)(2,1)}), bf16[8,256,128]{2,1,0:T(8,128)(2,1)S(1)}, u32[]{:S(2)}, u32[]{:S(2)}) async-start(bf16[8,256,128]{2,1,0:T(8,128)(2,1)} %bitcast.63), calls=%async_computation.5 | async-start | bytes 1048576 | tf_op jit(solution)/shard_map/all_to_all | solution.py:184
  282.5 3.2 %broadcast_multiply_fusion = f32[8,128,512]{2,1,0:T(8,128)} fusion(f32[8,128,512]{2,1,0:T(8,128)} %all-to-all-done.8), kind=kLoop, calls=%fused_computation.6 | loop fusion | flops 524288 | bytes 4194304 | tf_op jit(solution)/shard_map/mul | solution.py:203
  285.7 5.0 %all-to-all-done.5 = bf16[8,256,128]{2,1,0:T(8,128)(2,1)S(1)} async-done(((bf16[8,256,128]{2,1,0:T(8,128)(2,1)}), bf16[8,256,128]{2,1,0:T(8,128)(2,1)S(1)}, u32[]{:S(2)}, u32[]{:S(2)}) %all-to-all-start.5) | async-done | bytes 524320 | tf_op jit(solution)/shard_map/all_to_all | solution.py:184
  (63 shorter events, 27.2 us)
Async XLA Ops:
  0.6 104.6 %copy-start = (bf16[1024,512]{1,0:T(8,128)(2,1)S(1)}, bf16[1024,512]{1,0:T(8,128)(2,1)}, u32[]{:S(2)}) copy-start(bf16[1024,512]{1,0:T(8,128)(2,1)} %param.12) | copy-start | bytes 3145732
  0.6 8.7 %copy-start.7 = (s32[1,4]{1,0:T(1,128)S(1)}, s32[1,4]{1,0:T(1,128)}, u32[]{:S(2)}) copy-start(s32[1,4]{1,0:T(1,128)} %param.18) | copy-start | bytes 52
  0.7 9.3 %copy-start.6 = (s32[32,32,2]{1,2,0:T(2,128)S(1)}, s32[32,32,2]{1,2,0:T(2,128)}, u32[]{:S(2)}) copy-start(s32[32,32,2]{1,2,0:T(2,128)} %param.19) | copy-start | bytes 24580
  0.7 9.3 %copy-start.8 = (s32[1,32,2]{1,2,0:T(2,128)S(1)}, s32[1,32,2]{1,2,0:T(2,128)}, u32[]{:S(2)}) copy-start(s32[1,32,2]{1,2,0:T(2,128)} %param.20) | copy-start | bytes 772
  2.7 16.1 %all-to-all-start = ((bf16[256,8,128]{2,0,1:T(8,128)(2,1)}), bf16[256,8,128]{2,0,1:T(8,128)(2,1)S(1)}, u32[]{:S(2)}, u32[]{:S(2)}) async-start(bf16[256,8,128]{2,0,1:T(8,128)(2,1)} %copy_bitcast_fusion.1), calls=%async_computation | async-start | bytes 1048576 | tf_op jit(solution)/shard_map/all_to_all | solution.py:123
  18.8 2.1 copy-start.1
  21.0 12.6 %copy-start.10 = (s32[1,32,2]{1,2,0:T(2,128)S(1)}, s32[1,32,2]{1,2,0:T(2,128)}, u32[]{:S(2)}) copy-start(s32[1,32,2]{1,2,0:T(2,128)} %param.21) | copy-start | bytes 772
  21.0 59.2 %all-to-all-start.1 = ((bf16[32,2,128,128]{3,2,1,0:T(8,128)(2,1)}), bf16[32,2,128,128]{3,2,1,0:T(8,128)(2,1)S(1)}, u32[]{:S(2)}, u32[]{:S(2)}) async-start(bf16[32,2,128,128]{3,2,1,0:T(8,128)(2,1)} %bitcast.59), calls=%async_computation.1 | async-start | bytes 4194304 | tf_op jit(solution)/shard_map/all_to_all | solution.py:134
  80.2 1.3 copy-start.3
  89.9 15.3 %copy-start.9 = (f32[512]{0:T(512)S(1)}, f32[512]{0:T(512)}, u32[]{:S(2)}) copy-start(f32[512]{0:T(512)} %param.13) | copy-start | bytes 6148
  89.9 16.5 %copy-start.5 = (bf16[256,512]{1,0:T(8,128)(2,1)S(1)}, bf16[256,512]{1,0:T(8,128)(2,1)}, u32[]{:S(2)}) copy-start(bf16[256,512]{1,0:T(8,128)(2,1)} %param.14) | copy-start | bytes 786436
  106.7 30.1 %copy-start.4 = (bf16[16,128,128]{2,1,0:T(8,128)(2,1)S(1)}, bf16[16,128,128]{2,1,0:T(8,128)(2,1)}, u32[]{:S(2)}) copy-start(bf16[16,128,128]{2,1,0:T(8,128)(2,1)} %shard_map.139) | copy-start | bytes 1572868
  160.8 21.8 %all-to-all-start.7 = ((f32[32,5,512]{2,1,0:T(8,128)}), f32[32,5,512]{2,1,0:T(8,128)}, u32[]{:S(2)}, u32[]{:S(2)}) async-start(f32[32,5,512]{2,1,0:T(8,128)} %broadcast_in_dim.15), calls=%async_computation.7 | async-start | bytes 1048576 | tf_op jit(solution)/shard_map/all_to_all | solution.py:98
  182.7 60.0 %all-to-all-start.4 = ((bf16[32,2,136,128]{3,2,1,0:T(8,128)(2,1)}), bf16[32,2,136,128]{3,2,1,0:T(8,128)(2,1)S(1)}, u32[]{:S(2)}, u32[]{:S(2)}) async-start(bf16[32,2,136,128]{3,2,1,0:T(8,128)(2,1)} %pad_maximum_fusion), calls=%async_computation.4 | async-start | bytes 4456448 | tf_op jit(solution)/shard_map/all_to_all | solution.py:171
  242.7 19.1 %copy-start.2 = (bf16[32,2,136,128]{3,2,1,0:T(8,128)(2,1)}, bf16[32,2,136,128]{3,2,1,0:T(8,128)(2,1)S(1)}, u32[]{:S(2)}) copy-start(bf16[32,2,136,128]{3,2,1,0:T(8,128)(2,1)S(1)} %all-to-all-done.4) | copy-start | bytes 6684676
  244.5 32.4 %all-to-all-start.8 = ((f32[8,128,512]{2,1,0:T(8,128)}), f32[8,128,512]{2,1,0:T(8,128)}, u32[]{:S(2)}, u32[]{:S(2)}) async-start(f32[8,128,512]{2,1,0:T(8,128)} %broadcast_in_dim.16), calls=%async_computation.8 | async-start | bytes 4194304 | tf_op jit(solution)/shard_map/all_to_all | solution.py:193
  276.9 13.8 %all-to-all-start.5 = ((bf16[8,256,128]{2,1,0:T(8,128)(2,1)}), bf16[8,256,128]{2,1,0:T(8,128)(2,1)S(1)}, u32[]{:S(2)}, u32[]{:S(2)}) async-start(bf16[8,256,128]{2,1,0:T(8,128)(2,1)} %bitcast.63), calls=%async_computation.5 | async-start | bytes 1048576 | tf_op jit(solution)/shard_map/all_to_all | solution.py:184

commit v4 on v3

--- a/solution.py
+++ b/solution.py
@@ -30,6 +30,72 @@
         return carry
 
     lax.fori_loop(0, rows, row, 0)
+
+
+def _fwd_exchange_kernel(
+    domains, cols, banks, bank_ref, feat_ref, send_ref, acc_ref, recv_ref, send_sems, recv_sems, own_sem
+):
+    me = lax.axis_index("dom")
+    group = lax.axis_index("grp")
+    mesh_ids = pl.DeviceIdType.MESH
+
+    def remote(target, slot):
+        return pltpu.make_async_remote_copy(
+            src_ref=send_ref.at[target],
+            dst_ref=recv_ref.at[slot],
+            send_sem=send_sems.at[target],
+            recv_sem=recv_sems.at[slot],
+            device_id=(target, group),
+            device_id_type=mesh_ids,
+        )
+
+    barrier = pltpu.get_barrier_semaphore()
+
+    def greet(i, carry):
+        target = lax.rem(me + i, domains)
+        pl.semaphore_signal(barrier, 1, device_id=(target, group), device_id_type=mesh_ids)
+        return carry
+
+    lax.fori_loop(1, domains, greet, 0)
+    pl.semaphore_wait(barrier, domains - 1)
+
+    def send(i, carry):
+        remote(lax.rem(me + i, domains), me).start()
+        return carry
+
+    lax.fori_loop(1, domains, send, 0)
+    own = pltpu.make_async_copy(send_ref.at[me], recv_ref.at[me], own_sem)
+    own.start()
+    _fwd_local_kernel(cols, banks, bank_ref, feat_ref, acc_ref)
+    own.wait()
+
+    def finish(i, carry):
+        remote(lax.rem(me + i, domains), me).wait_send()
+        remote(me, lax.rem(me + domains - i, domains)).wait_recv()
+        return carry
+
+    lax.fori_loop(1, domains, finish, 0)
+
+
+def _fwd_exchange(cols, banks, bank, blocks, send):
+    n, tile, width = blocks.shape
+    domains = send.shape[0]
+    return pl.pallas_call(
+        functools.partial(_fwd_exchange_kernel, domains),
+        out_shape=(
+            jax.ShapeDtypeStruct((n, tile, width), jnp.float32),
+            jax.ShapeDtypeStruct(send.shape, send.dtype),
+        ),
+        in_specs=[_SMEM, _SMEM, _VMEM, _VMEM, pl.BlockSpec(memory_space=pl.ANY)],
+        out_specs=(_VMEM, pl.BlockSpec(memory_space=pl.ANY)),
+        scratch_shapes=[
+            pltpu.SemaphoreType.DMA((domains,)),
+            pltpu.SemaphoreType.DMA((domains,)),
+            pltpu.SemaphoreType.DMA,
+        ],
+        compiler_params=pltpu.CompilerParams(collective_id=0, has_side_effects=True),
+        cost_estimate=_cost(cols.size, tile, 2 * bank.size + 6 * blocks.size + 4 * send.size),
+    )(cols, banks, bank, blocks, send)
 
 
 def _bwd_local_kernel(cols, banks, bank_t_ref, grad_ref, acc_ref):
@@ -131,12 +197,13 @@
 
     outgoing = lax.dynamic_index_in_dim(send_table, domain_index, 0, keepdims=False)
     send_ids = own_pub[jnp.maximum(outgoing, 0)]
-    remote = lax.all_to_all(feat_blocks[send_ids], "dom", 0, 0, tiled=True)
     incoming = lax.dynamic_index_in_dim(send_table, domain_index, 1, keepdims=False)
     live_in = (incoming >= 0).astype(jnp.int32).reshape(-1)
     rows_in = halo_rows[0]
 
-    local_acc = _local(_fwd_local_kernel, cols_here, banks_here, tile_bank, feat_blocks)
+    local_acc, remote = _fwd_exchange(
+        cols_here, banks_here, tile_bank, feat_blocks, feat_blocks[send_ids]
+    )
     agg_blocks = _halo(
         rows_in.reshape(-1),
         halo_banks[0].reshape(-1),

time: 293 us -> 291 us (level)
  Pallas kernels: 34 us -> 85.5 us
  waiting for transfers between devices: 109 us -> 67.5 us
  starting transfers between devices: 43.4 us -> 32.9 us
    pallas_call x0 -> x1, Pallas kernels: none -> 58.3 us  [_fwd_exchange(): pl.pallas_call(functools.partial(_fwd_exchange_kernel, domains), out_shap...]
    all_to_all x1 -> x0, waiting for transfers between devices: 39 us -> none  [per_device(): remote = lax.all_to_all(feat_blocks[send_ids], 'dom', 0, 0, tiled=True)]
    all_to_all x1 -> x0, starting transfers between devices: 10.5 us -> none  [per_device(): remote = lax.all_to_all(feat_blocks[send_ids], 'dom', 0, 0, tiled=True)]
    pallas_call x2 -> x1, Pallas kernels: 14 us -> 7.11 us  [_local(): pl.pallas_call(kernel, out_shape=jax.ShapeDtypeStruct((n, tile, width), j...]
  transfers between devices with their start and end apart: 6 -> 5, of which waited for: 6 -> 5; matrix products, arithmetic and copies ran while one was open for 9% -> 9% of each run, Pallas kernels for 9% -> 6%
where the time goes in v4:
time: 291 us; the launch traced here: 290 us
  Pallas kernels  85.5 us (29%)
  waiting for transfers between devices  67.5 us (23%)
  blocking collectives  65.2 us (22%)
  starting transfers between devices  32.9 us (11%)
  local copies, waits for them, and re-layouts  22.2 us (8%)
  other arithmetic  12.9 us (4%)
  matrix products  3.14 us (1%)
    pallas_call x1, Pallas kernels, _fwd_exchange(): pl.pallas_call(functools.partial(_fwd_exchange_kernel, domains), out_shap...  58.3 us
    all_to_all x1, waiting for transfers between devices, per_device(): back_in = lax.all_to_all(payload, 'dom', 0, 0, tiled=True)  49.3 us
    all_to_all x1, blocking collectives, per_device(): lax.all_to_all(jnp.broadcast_to(grad_pre[None], (groups,) + grad_pre.shap...  30.1 us
    all_to_all x1, blocking collectives, _dom_sum(): lax.all_to_all(y.reshape(domains, piece, width), 'dom', 0, 0, tiled=True)  22.2 us
    pallas_call x2, Pallas kernels, _halo(): pl.pallas_call(_halo_kernel, out_shape=jax.ShapeDtypeStruct((n, tile, wid...  20.2 us
    all_to_all x1, blocking collectives, per_device(): lax.all_to_all(agg_narrow, 'grp', split_axis=0, concat_axis=1, tiled=True)  12.8 us
    all_to_all x1, waiting for transfers between devices, _dom_sum(): lax.all_to_all(jnp.broadcast_to(z[None], (domains, piece, width)), 'dom',...  8.17 us
    all_to_all x1, starting transfers between devices, _dom_sum(): lax.all_to_all(jnp.broadcast_to(z[None], (domains, piece, width)), 'dom',...  8.1 us
  transfers between devices with their start and end apart: 5, of which 5 were waited for; matrix products, arithmetic and copies ran while one was open for 9% of the time, Pallas kernels for 6%

profile of v4, /device:TPU:1, one launch (start us, length us, event | category | flops | bytes accessed | tf_op | source)
XLA Modules:
  0.0 290.1 jit_solution(8511058408666761145)
XLA Ops:
  0.7 2.0 copy_bitcast_fusion.1
  2.7 6.6 %all-to-all-start = ((bf16[256,8,128]{2,0,1:T(8,128)(2,1)}), bf16[256,8,128]{2,0,1:T(8,128)(2,1)S(1)}, u32[]{:S(2)}, u32[]{:S(2)}) async-start(bf16[256,8,128]{2,0,1:T(8,128)(2,1)} %copy_bitcast_fusion.1), calls=%async_computation | async-start | bytes 1048576 | tf_op jit(solution)/shard_map/all_to_all | solution.py:189
  10.0 2.6 compare_select_fusion.1
  15.5 3.3 %all-to-all-done = bf16[256,8,128]{2,0,1:T(8,128)(2,1)S(1)} async-done(((bf16[256,8,128]{2,0,1:T(8,128)(2,1)}), bf16[256,8,128]{2,0,1:T(8,128)(2,1)S(1)}, u32[]{:S(2)}, u32[]{:S(2)}) %all-to-all-start) | async-done | bytes 524320 | tf_op jit(solution)/shard_map/all_to_all | solution.py:189
  18.8 2.1 gather_fusion
  21.0 58.3 %shard_map.138 = (f32[16,128,128]{2,1,0:T(8,128)}, bf16[32,2,128,128]{3,2,1,0:T(8,128)(2,1)}) custom-call(s32[16,16]{1,0:T(8,128)} %bitcast.70, s32[16,16]{1,0:T(8,128)} %bitcast.72, bf16[16,128,128]{2,1,0:T(8,128)(2,1)} %bank_ref.3, bf16[16,128,128]{2,1,0:T(8,128)(2,1)} %bitcast.54, bf16[32,2,128,128]{3,2,1,0:T(8,128)(2,1)} %bitcast.66), custom_call_target="tpu_custom_call" | custom-call | flops 1073741824 | bytes 6291456 | tf_op jit(solution)/shard_map/pallas_call | solution.py:83
  79.2 8.6 %shard_map.139 = bf16[16,128,128]{2,1,0:T(8,128)(2,1)} custom-call(s32[64]{0:T(128)} %reshape_squeeze.6.dest, s32[64]{0:T(128)} %reshape_squeeze.7.banks, s32[64]{0:T(128)} %reshape.141.live, bf16[16,128,128]{2,1,0:T(8,128)(2,1)} %bank_ref.3, f32[16,128,128]{2,1,0:T(8,128)} %get-tuple-element.6.acc_in, bf16[64,128,128]{2,1,0:T(8,128)(2,1)} %bitcast.61), custom_call_target="tpu_custom_call" | custom-call | flops 268435456 | bytes 4194304 | tf_op jit(solution)/shard_map/pallas_call | solution.py:148
  89.1 12.8 %all_to_all.79 = bf16[8,256,128]{1,2,0:T(8,128)(2,1)S(1)} all-to-all(bf16[8,256,128]{1,2,0:T(8,128)(2,1)S(1)} %copy.55), channel_id=1, replica_groups=mesh['dom'=32,'grp'=8] {'grp'}, dimensions={0} | all-to-all | bytes 1048576 | tf_op jit(solution)/shard_map/all_to_all | solution.py:216
  103.4 30.1 %all_to_all.80 = bf16[8,256,512]{2,1,0:T(8,128)(2,1)S(1)} all-to-all(bf16[8,256,512]{2,1,0:T(8,128)(2,1)S(1)} %broadcast_in_dim.12), channel_id=1, replica_groups=mesh['dom'=32,'grp'=8] {'grp'}, dimensions={0} | all-to-all | bytes 4194304 | tf_op jit(solution)/shard_map/all_to_all | solution.py:220
  135.1 22.2 %all_to_all.81 = f32[32,5,512]{2,1,0:T(8,128)} all-to-all(f32[32,5,512]{2,1,0:T(8,128)} %reshape.139), channel_id=1, replica_groups=mesh['dom'=32,'grp'=8] {'dom'}, dimensions={0} | all-to-all | bytes 655360 | tf_op jit(solution)/shard_map/all_to_all | solution.py:163
  159.3 8.1 %all-to-all-start.6 = ((f32[32,5,512]{2,1,0:T(8,128)}), f32[32,5,512]{2,1,0:T(8,128)}, u32[]{:S(2)}, u32[]{:S(2)}) async-start(f32[32,5,512]{2,1,0:T(8,128)} %broadcast_in_dim.15), calls=%async_computation.6 | async-start | bytes 1048576 | tf_op jit(solution)/shard_map/all_to_all | solution.py:164
  169.3 2.0 gather_fusion.1
  173.0 8.2 %all-to-all-done.6 = f32[32,5,512]{2,1,0:T(8,128)} async-done(((f32[32,5,512]{2,1,0:T(8,128)}), f32[32,5,512]{2,1,0:T(8,128)}, u32[]{:S(2)}, u32[]{:S(2)}) %all-to-all-start.6) | async-done | bytes 327712 | tf_op jit(solution)/shard_map/all_to_all | solution.py:164
  181.2 7.9 %all-to-all-start.3 = ((bf16[32,2,136,128]{3,2,1,0:T(8,128)(2,1)}), bf16[32,2,136,128]{3,2,1,0:T(8,128)(2,1)S(1)}, u32[]{:S(2)}, u32[]{:S(2)}) async-start(bf16[32,2,136,128]{3,2,1,0:T(8,128)(2,1)} %pad_maximum_fusion), calls=%async_computation.3 | async-start | bytes 4456448 | tf_op jit(solution)/shard_map/all_to_all | solution.py:238
  189.1 1.8 reshape.140
  191.9 49.3 %all-to-all-done.3 = bf16[32,2,136,128]{3,2,1,0:T(8,128)(2,1)S(1)} async-done(((bf16[32,2,136,128]{3,2,1,0:T(8,128)(2,1)}), bf16[32,2,136,128]{3,2,1,0:T(8,128)(2,1)S(1)}, u32[]{:S(2)}, u32[]{:S(2)}) %all-to-all-start.3) | async-done | bytes 2228256 | tf_op jit(solution)/shard_map/all_to_all | solution.py:238
  241.2 1.8 broadcast_in_dim.16
  243.0 6.0 %all-to-all-start.7 = ((f32[8,128,512]{2,1,0:T(8,128)}), f32[8,128,512]{2,1,0:T(8,128)}, u32[]{:S(2)}, u32[]{:S(2)}) async-start(f32[8,128,512]{2,1,0:T(8,128)} %broadcast_in_dim.16), calls=%async_computation.7 | async-start | bytes 4194304 | tf_op jit(solution)/shard_map/all_to_all | solution.py:260
  249.0 2.1 copy.60
  253.2 7.1 %shard_map.140.acc_in = f32[16,128,128]{2,1,0:T(8,128)} custom-call(s32[16,16]{1,0:T(8,128)} %bitcast.71, s32[16,16]{1,0:T(8,128)} %bitcast.73, bf16[16,128,128]{2,1,0:T(8,128)(2,1)} %bitcast.63, bf16[16,128,128]{2,1,0:T(8,128)(2,1)} %bitcast.56), custom_call_target="tpu_custom_call" | custom-call | flops 1073741824 | bytes 2097152 | tf_op jit(solution)/shard_map/pallas_call | solution.py:137
  262.1 11.6 %shard_map.141 = bf16[16,128,128]{2,1,0:T(8,128)(2,1)} custom-call(s32[64]{0:T(128)} %reshape.134.dest, s32[64]{0:T(128)} %reshape.142.banks, s32[64]{0:T(128)} %reshape.143.live, bf16[16,128,128]{2,1,0:T(8,128)(2,1)} %bitcast.64, f32[16,128,128]{2,1,0:T(8,128)} %shard_map.140.acc_in, bf16[64,136,128]{2,1,0:T(8,128)(2,1)} %bitcast.57), custom_call_target="tpu_custom_call" | custom-call | flops 268435456 | bytes 4325376 | tf_op jit(solution)/shard_map/pallas_call | solution.py:148
  275.4 4.3 %all-to-all-start.4 = ((bf16[8,256,128]{2,1,0:T(8,128)(2,1)}), bf16[8,256,128]{2,1,0:T(8,128)(2,1)S(1)}, u32[]{:S(2)}, u32[]{:S(2)}) async-start(bf16[8,256,128]{2,1,0:T(8,128)(2,1)} %bitcast.62), calls=%async_computation.4 | async-start | bytes 1048576 | tf_op jit(solution)/shard_map/all_to_all | solution.py:251
  281.0 3.2 %broadcast_multiply_fusion = f32[8,128,512]{2,1,0:T(8,128)} fusion(f32[8,128,512]{2,1,0:T(8,128)} %all-to-all-done.7), kind=kLoop, calls=%fused_computation.6 | loop fusion | flops 524288 | bytes 4194304 | tf_op jit(solution)/shard_map/mul | solution.py:270
  284.2 5.0 %all-to-all-done.4 = bf16[8,256,128]{2,1,0:T(8,128)(2,1)S(1)} async-done(((bf16[8,256,128]{2,1,0:T(8,128)(2,1)}), bf16[8,256,128]{2,1,0:T(8,128)(2,1)S(1)}, u32[]{:S(2)}, u32[]{:S(2)}) %all-to-all-start.4) | async-done | bytes 524320 | tf_op jit(solution)/shard_map/all_to_all | solution.py:251
  (59 shorter events, 22.2 us)
Async XLA Ops:
  0.6 101.3 %copy-start = (bf16[1024,512]{1,0:T(8,128)(2,1)S(1)}, bf16[1024,512]{1,0:T(8,128)(2,1)}, u32[]{:S(2)}) copy-start(bf16[1024,512]{1,0:T(8,128)(2,1)} %param.12) | copy-start | bytes 3145732
  0.6 8.7 %copy-start.7 = (s32[1,32,2]{1,2,0:T(2,128)S(1)}, s32[1,32,2]{1,2,0:T(2,128)}, u32[]{:S(2)}) copy-start(s32[1,32,2]{1,2,0:T(2,128)} %param.20) | copy-start | bytes 772
  0.7 8.8 %copy-start.6 = (s32[1,4]{1,0:T(1,128)S(1)}, s32[1,4]{1,0:T(1,128)}, u32[]{:S(2)}) copy-start(s32[1,4]{1,0:T(1,128)} %param.18) | copy-start | bytes 52
  0.7 9.4 %copy-start.5 = (s32[32,32,2]{1,2,0:T(2,128)S(1)}, s32[32,32,2]{1,2,0:T(2,128)}, u32[]{:S(2)}) copy-start(s32[32,32,2]{1,2,0:T(2,128)} %param.19) | copy-start | bytes 24580
  0.7 14.1 %copy-start.9 = (s32[1,32,2]{1,2,0:T(2,128)S(1)}, s32[1,32,2]{1,2,0:T(2,128)}, u32[]{:S(2)}) copy-start(s32[1,32,2]{1,2,0:T(2,128)} %param.21) | copy-start | bytes 772
  2.7 16.1 %all-to-all-start = ((bf16[256,8,128]{2,0,1:T(8,128)(2,1)}), bf16[256,8,128]{2,0,1:T(8,128)(2,1)S(1)}, u32[]{:S(2)}, u32[]{:S(2)}) async-start(bf16[256,8,128]{2,0,1:T(8,128)(2,1)} %copy_bitcast_fusion.1), calls=%async_computation | async-start | bytes 1048576 | tf_op jit(solution)/shard_map/all_to_all | solution.py:189
  18.8 2.1 copy-start.1
  87.8 14.1 %copy-start.8 = (f32[512]{0:T(512)S(1)}, f32[512]{0:T(512)}, u32[]{:S(2)}) copy-start(f32[512]{0:T(512)} %param.13) | copy-start | bytes 6148
  87.8 15.3 %copy-start.4 = (bf16[256,512]{1,0:T(8,128)(2,1)S(1)}, bf16[256,512]{1,0:T(8,128)(2,1)}, u32[]{:S(2)}) copy-start(bf16[256,512]{1,0:T(8,128)(2,1)} %param.14) | copy-start | bytes 786436
  103.4 30.1 %copy-start.3 = (bf16[16,128,128]{2,1,0:T(8,128)(2,1)S(1)}, bf16[16,128,128]{2,1,0:T(8,128)(2,1)}, u32[]{:S(2)}) copy-start(bf16[16,128,128]{2,1,0:T(8,128)(2,1)} %shard_map.139) | copy-start | bytes 1572868
  159.3 21.8 %all-to-all-start.6 = ((f32[32,5,512]{2,1,0:T(8,128)}), f32[32,5,512]{2,1,0:T(8,128)}, u32[]{:S(2)}, u32[]{:S(2)}) async-start(f32[32,5,512]{2,1,0:T(8,128)} %broadcast_in_dim.15), calls=%async_computation.6 | async-start | bytes 1048576 | tf_op jit(solution)/shard_map/all_to_all | solution.py:164
  181.2 60.0 %all-to-all-start.3 = ((bf16[32,2,136,128]{3,2,1,0:T(8,128)(2,1)}), bf16[32,2,136,128]{3,2,1,0:T(8,128)(2,1)S(1)}, u32[]{:S(2)}, u32[]{:S(2)}) async-start(bf16[32,2,136,128]{3,2,1,0:T(8,128)(2,1)} %pad_maximum_fusion), calls=%async_computation.3 | async-start | bytes 4456448 | tf_op jit(solution)/shard_map/all_to_all | solution.py:238
  241.2 19.0 %copy-start.2 = (bf16[32,2,136,128]{3,2,1,0:T(8,128)(2,1)}, bf16[32,2,136,128]{3,2,1,0:T(8,128)(2,1)S(1)}, u32[]{:S(2)}) copy-start(bf16[32,2,136,128]{3,2,1,0:T(8,128)(2,1)S(1)} %all-to-all-done.3) | copy-start | bytes 6684676
  243.0 32.4 %all-to-all-start.7 = ((f32[8,128,512]{2,1,0:T(8,128)}), f32[8,128,512]{2,1,0:T(8,128)}, u32[]{:S(2)}, u32[]{:S(2)}) async-start(f32[8,128,512]{2,1,0:T(8,128)} %broadcast_in_dim.16), calls=%async_computation.7 | async-start | bytes 4194304 | tf_op jit(solution)/shard_map/all_to_all | solution.py:260
  275.4 13.8 %all-to-all-start.4 = ((bf16[8,256,128]{2,1,0:T(8,128)(2,1)}), bf16[8,256,128]{2,1,0:T(8,128)(2,1)S(1)}, u32[]{:S(2)}, u32[]{:S(2)}) async-start(bf16[8,256,128]{2,1,0:T(8,128)(2,1)} %bitcast.62), calls=%async_computation.4 | async-start | bytes 1048576 | tf_op jit(solution)/shard_map/all_to_all | solution.py:251

commit v5 on v4

--- a/solution.py
+++ b/solution.py
@@ -235,8 +235,22 @@
         halo_banks[0].astype(jnp.bfloat16)[:, :, None, None], (domains, slot_count, 8, narrow)
     )
     payload = jnp.concatenate([grad_blocks[rows_in], bank_rows], axis=2)
-    back_in = lax.all_to_all(payload, "dom", 0, 0, tiled=True)
+    halo_rows_sent = slot_count * (tile_size + 8)
+    partial = jnp.concatenate([weight_part, bias_part[None]], axis=0)
+    kept_rows, width = partial.shape
+    piece = -(-kept_rows // domains)
+    pieces = jnp.pad(partial, ((0, piece * domains - kept_rows), (0, 0))).reshape(
+        domains, piece, width
+    )
+    high = pieces.astype(jnp.bfloat16)
+    low = (pieces - high.astype(jnp.float32)).astype(jnp.bfloat16)
+    split = jnp.stack([high, low], axis=1).reshape(domains, -1, narrow)
+    mixed = jnp.concatenate([payload.reshape(domains, halo_rows_sent, narrow), split], axis=1)
+    arrived = lax.all_to_all(mixed, "dom", 0, 0, tiled=True)
+    back_in = arrived[:, :halo_rows_sent].reshape(domains, slot_count, tile_size + 8, narrow)
     banks_back = back_in[:, :, tile_size, 0].astype(jnp.int32)
+    parts_in = arrived[:, halo_rows_sent:].reshape(domains, 2, piece, width).astype(jnp.float32)
+    reduced = (parts_in[:, 0] + parts_in[:, 1]).sum(0)
     live_out = (outgoing >= 0).astype(jnp.int32).reshape(-1)
 
     local_back = _local(_bwd_local_kernel, cols_here, banks_here, bank_t, grad_blocks)
@@ -256,7 +270,9 @@
         tiled=True,
     )
     norm_scale = float(rows_here * groups * domains) ** (-0.5)
-    summed = _dom_sum(jnp.concatenate([weight_part, bias_part[None]], axis=0))
+    summed = lax.all_to_all(
+        jnp.broadcast_to(reduced[None], (domains, piece, width)), "dom", 0, 0, tiled=True
+    ).reshape(domains * piece, width)
     weight_total = lax.all_to_all(
         jnp.broadcast_to(summed[None, :narrow], (groups, narrow, summed.shape[1])),
         "grp",

time: 291 us -> 295 us (1.014)
  blocking collectives: 65.2 us -> 78.6 us
  waiting for transfers between devices: 67.5 us -> 61.7 us
  local copies, waits for them, and re-layouts: 22.2 us -> 27.2 us
  starting transfers between devices: 32.9 us -> 28.4 us
  other arithmetic: 12.9 us -> 8.95 us
    all_to_all x2, waiting for transfers between devices: 57.5 us -> 26 us  [the longest x1 26 us: per_device(): lax.all_to_all(jnp.broadcast_to(grad_pre[None], (groups,) + grad_pre.shap...]
    all_to_all x1, waiting for transfers between devices: 1.69 us -> 23.9 us  [per_device(): lax.all_to_all(jnp.broadcast_to(summed[None, :narrow], (groups, narrow, s...]
    all_to_all x2 -> x1, blocking collectives: 52.3 us -> 65.7 us  [per_device(): arrived = lax.all_to_all(mixed, 'dom', 0, 0, tiled=True)]
    all_to_all x1, waiting for transfers between devices: 4.96 us -> 8.37 us  [per_device(): lax.all_to_all(grad_total.reshape(part_rows, narrow), 'grp', split_axis=0...]
    all_to_all x2, starting transfers between devices: 16 us -> 12.9 us  [the longest x1 8.33 us: per_device(): lax.all_to_all(jnp.broadcast_to(reduced[None], (domains, piece, width)),...]
  transfers between devices with their start and end apart: 5 -> 5, of which waited for: 5 -> 4; matrix products, arithmetic and copies ran while one was open for 9% -> 5% of each run, Pallas kernels for 6% -> 6%
where the time goes in v5:
time: 295 us; the launch traced here: 294 us
  Pallas kernels  84.2 us (29%)
  blocking collectives  78.6 us (27%)
  waiting for transfers between devices  61.7 us (21%)
  starting transfers between devices  28.4 us (10%)
  local copies, waits for them, and re-layouts  27.2 us (9%)
  other arithmetic  8.95 us (3%)
  matrix products  4.18 us (1%)
    all_to_all x1, blocking collectives, per_device(): arrived = lax.all_to_all(mixed, 'dom', 0, 0, tiled=True)  65.7 us
    pallas_call x1, Pallas kernels, _fwd_exchange(): pl.pallas_call(functools.partial(_fwd_exchange_kernel, domains), out_shap...  58.3 us
    all_to_all x1, waiting for transfers between devices, per_device(): lax.all_to_all(jnp.broadcast_to(grad_pre[None], (groups,) + grad_pre.shap...  26 us
    all_to_all x1, waiting for transfers between devices, per_device(): lax.all_to_all(jnp.broadcast_to(summed[None, :narrow], (groups, narrow, s...  23.9 us
    pallas_call x2, Pallas kernels, _halo(): pl.pallas_call(_halo_kernel, out_shape=jax.ShapeDtypeStruct((n, tile, wid...  18.8 us
    all_to_all x1, blocking collectives, per_device(): lax.all_to_all(agg_narrow, 'grp', split_axis=0, concat_axis=1, tiled=True)  12.8 us
    all_to_all x1, waiting for transfers between devices, per_device(): lax.all_to_all(grad_total.reshape(part_rows, narrow), 'grp', split_axis=0...  8.37 us
    all_to_all x1, starting transfers between devices, per_device(): lax.all_to_all(jnp.broadcast_to(reduced[None], (domains, piece, width)),...  8.33 us
  transfers between devices with their start and end apart: 5, of which 4 were waited for; matrix products, arithmetic and copies ran while one was open for 5% of the time, Pallas kernels for 6%

profile of v5, /device:TPU:1, one launch (start us, length us, event | category | flops | bytes accessed | tf_op | source)
XLA Modules:
  0.0 294.0 jit_solution(9742674340414507529)
XLA Ops:
  0.7 2.0 copy_bitcast_fusion.1
  2.7 6.6 %all-to-all-start = ((bf16[256,8,128]{2,0,1:T(8,128)(2,1)}), bf16[256,8,128]{2,0,1:T(8,128)(2,1)S(1)}, u32[]{:S(2)}, u32[]{:S(2)}) async-start(bf16[256,8,128]{2,0,1:T(8,128)(2,1)} %copy_bitcast_fusion.1), calls=%async_computation | async-start | bytes 1048576 | tf_op jit(solution)/shard_map/all_to_all | solution.py:189
  12.7 2.5 compare_select_fusion.1
  15.4 3.4 %all-to-all-done = bf16[256,8,128]{2,0,1:T(8,128)(2,1)S(1)} async-done(((bf16[256,8,128]{2,0,1:T(8,128)(2,1)}), bf16[256,8,128]{2,0,1:T(8,128)(2,1)S(1)}, u32[]{:S(2)}, u32[]{:S(2)}) %all-to-all-start) | async-done | bytes 524320 | tf_op jit(solution)/shard_map/all_to_all | solution.py:189
  18.8 2.1 gather_fusion
  21.0 58.3 %shard_map.138 = (f32[16,128,128]{2,1,0:T(8,128)}, bf16[32,2,128,128]{3,2,1,0:T(8,128)(2,1)}) custom-call(s32[16,16]{1,0:T(8,128)} %bitcast.74, s32[16,16]{1,0:T(8,128)} %bitcast.76, bf16[16,128,128]{2,1,0:T(8,128)(2,1)} %bank_ref.3, bf16[16,128,128]{2,1,0:T(8,128)(2,1)} %bitcast.56, bf16[32,2,128,128]{3,2,1,0:T(8,128)(2,1)} %bitcast.70), custom_call_target="tpu_custom_call" | custom-call | flops 1073741824 | bytes 6291456 | tf_op jit(solution)/shard_map/pallas_call | solution.py:83
  79.2 7.2 %shard_map.139 = bf16[16,128,128]{2,1,0:T(8,128)(2,1)} custom-call(s32[64]{0:T(128)} %reshape_squeeze.6.dest, s32[64]{0:T(128)} %reshape_squeeze.7.banks, s32[64]{0:T(128)} %reshape.182.live, bf16[16,128,128]{2,1,0:T(8,128)(2,1)} %bank_ref.3, f32[16,128,128]{2,1,0:T(8,128)} %get-tuple-element.6.acc_in, bf16[64,128,128]{2,1,0:T(8,128)(2,1)} %bitcast.65), custom_call_target="tpu_custom_call" | custom-call | flops 268435456 | bytes 4194304 | tf_op jit(solution)/shard_map/pallas_call | solution.py:148
  87.7 12.8 %all_to_all.74 = bf16[8,256,128]{1,2,0:T(8,128)(2,1)S(1)} all-to-all(bf16[8,256,128]{1,2,0:T(8,128)(2,1)S(1)} %copy.42), channel_id=1, replica_groups=mesh['dom'=32,'grp'=8] {'grp'}, dimensions={0} | all-to-all | bytes 1048576 | tf_op jit(solution)/shard_map/all_to_all | solution.py:216
  103.3 4.5 %all-to-all-start.2 = ((bf16[8,256,512]{2,1,0:T(8,128)(2,1)}), bf16[8,256,512]{2,1,0:T(8,128)(2,1)S(1)}, u32[]{:S(2)}, u32[]{:S(2)}) async-start(bf16[8,256,512]{2,1,0:T(8,128)(2,1)} %broadcast_in_dim.12), calls=%async_computation.2 | async-start | bytes 4194304 | tf_op jit(solution)/shard_map/all_to_all | solution.py:220
  108.2 26.0 %all-to-all-done.2 = bf16[8,256,512]{2,1,0:T(8,128)(2,1)S(1)} async-done(((bf16[8,256,512]{2,1,0:T(8,128)(2,1)}), bf16[8,256,512]{2,1,0:T(8,128)(2,1)S(1)}, u32[]{:S(2)}, u32[]{:S(2)}) %all-to-all-start.2) | async-done | bytes 2097184 | tf_op jit(solution)/shard_map/all_to_all | solution.py:220
  134.2 1.5 fusion.6
  142.1 2.0 gather_fusion.1
  144.6 65.7 %all_to_all.75 = bf16[32,312,128]{2,1,0:T(8,128)(2,1)S(1)} all-to-all(bf16[32,312,128]{2,1,0:T(8,128)(2,1)S(1)} %pad_maximum_fusion), channel_id=1, replica_groups=mesh['dom'=32,'grp'=8] {'dom'}, dimensions={0} | all-to-all | bytes 5111808 | tf_op jit(solution)/shard_map/all_to_all | solution.py:249
  213.0 8.3 %all-to-all-start.5 = ((f32[32,5,512]{2,1,0:T(8,128)}), f32[32,5,512]{2,1,0:T(8,128)}, u32[]{:S(2)}, u32[]{:S(2)}) async-start(f32[32,5,512]{2,1,0:T(8,128)} %broadcast_in_dim.15), calls=%async_computation.5 | async-start | bytes 1048576 | tf_op jit(solution)/shard_map/all_to_all | solution.py:273
  223.7 7.1 %shard_map.140.acc_in = f32[16,128,128]{2,1,0:T(8,128)} custom-call(s32[16,16]{1,0:T(8,128)} %bitcast.75, s32[16,16]{1,0:T(8,128)} %bitcast.77, bf16[16,128,128]{2,1,0:T(8,128)(2,1)} %bitcast.66, bf16[16,128,128]{2,1,0:T(8,128)(2,1)} %bitcast.58), custom_call_target="tpu_custom_call" | custom-call | flops 1073741824 | bytes 2097152 | tf_op jit(solution)/shard_map/pallas_call | solution.py:137
  230.8 1.8 slice.42
  234.5 11.6 %shard_map.141 = bf16[16,128,128]{2,1,0:T(8,128)(2,1)} custom-call(s32[64]{0:T(128)} %reshape.173.dest, s32[64]{0:T(128)} %reshape.183.banks, s32[64]{0:T(128)} %reshape.184.live, bf16[16,128,128]{2,1,0:T(8,128)(2,1)} %bitcast.67, f32[16,128,128]{2,1,0:T(8,128)} %shard_map.140.acc_in, bf16[64,136,128]{2,1,0:T(8,128)(2,1)} %bitcast.60), custom_call_target="tpu_custom_call" | custom-call | flops 268435456 | bytes 4325376 | tf_op jit(solution)/shard_map/pallas_call | solution.py:148
  246.1 4.5 %all-to-all-start.4 = ((bf16[8,256,128]{2,1,0:T(8,128)(2,1)}), bf16[8,256,128]{2,1,0:T(8,128)(2,1)S(1)}, u32[]{:S(2)}, u32[]{:S(2)}) async-start(bf16[8,256,128]{2,1,0:T(8,128)(2,1)} %bitcast.68), calls=%async_computation.4 | async-start | bytes 1048576 | tf_op jit(solution)/shard_map/all_to_all | solution.py:265
  251.8 8.4 %all-to-all-done.4 = bf16[8,256,128]{2,1,0:T(8,128)(2,1)S(1)} async-done(((bf16[8,256,128]{2,1,0:T(8,128)(2,1)}), bf16[8,256,128]{2,1,0:T(8,128)(2,1)S(1)}, u32[]{:S(2)}, u32[]{:S(2)}) %all-to-all-start.4) | async-done | bytes 524320 | tf_op jit(solution)/shard_map/all_to_all | solution.py:265
  260.1 1.6 broadcast_in_dim.16
  261.7 4.4 %all-to-all-start.6 = ((f32[8,128,512]{2,1,0:T(8,128)}), f32[8,128,512]{2,1,0:T(8,128)S(1)}, u32[]{:S(2)}, u32[]{:S(2)}) async-start(f32[8,128,512]{2,1,0:T(8,128)} %broadcast_in_dim.16), calls=%async_computation.6 | async-start | bytes 4194304 | tf_op jit(solution)/shard_map/all_to_all | solution.py:276
  266.1 1.9 copy_bitcast_fusion
  268.6 23.9 %all-to-all-done.6 = f32[8,128,512]{2,1,0:T(8,128)S(1)} async-done(((f32[8,128,512]{2,1,0:T(8,128)}), f32[8,128,512]{2,1,0:T(8,128)S(1)}, u32[]{:S(2)}, u32[]{:S(2)}) %all-to-all-start.6) | async-done | bytes 2097184 | tf_op jit(solution)/shard_map/all_to_all | solution.py:276
  292.4 1.6 broadcast_multiply_fusion
  (70 shorter events, 23.4 us)
Async XLA Ops:
  0.6 99.9 %copy-start = (bf16[1024,512]{1,0:T(8,128)(2,1)S(1)}, bf16[1024,512]{1,0:T(8,128)(2,1)}, u32[]{:S(2)}) copy-start(bf16[1024,512]{1,0:T(8,128)(2,1)} %param.12) | copy-start | bytes 3145732
  0.6 8.7 %copy-start.9 = (s32[1,32,2]{1,2,0:T(2,128)S(1)}, s32[1,32,2]{1,2,0:T(2,128)}, u32[]{:S(2)}) copy-start(s32[1,32,2]{1,2,0:T(2,128)} %param.20) | copy-start | bytes 772
  0.7 9.4 %copy-start.11 = (s32[1,32,2]{1,2,0:T(2,128)S(1)}, s32[1,32,2]{1,2,0:T(2,128)}, u32[]{:S(2)}) copy-start(s32[1,32,2]{1,2,0:T(2,128)} %param.21) | copy-start | bytes 772
  0.7 10.1 %copy-start.7 = (s32[32,32,2]{1,2,0:T(2,128)S(1)}, s32[32,32,2]{1,2,0:T(2,128)}, u32[]{:S(2)}) copy-start(s32[32,32,2]{1,2,0:T(2,128)} %param.19) | copy-start | bytes 24580
  0.7 11.4 %copy-start.8 = (s32[1,4]{1,0:T(1,128)S(1)}, s32[1,4]{1,0:T(1,128)}, u32[]{:S(2)}) copy-start(s32[1,4]{1,0:T(1,128)} %param.18) | copy-start | bytes 52
  2.7 16.1 %all-to-all-start = ((bf16[256,8,128]{2,0,1:T(8,128)(2,1)}), bf16[256,8,128]{2,0,1:T(8,128)(2,1)S(1)}, u32[]{:S(2)}, u32[]{:S(2)}) async-start(bf16[256,8,128]{2,0,1:T(8,128)(2,1)} %copy_bitcast_fusion.1), calls=%async_computation | async-start | bytes 1048576 | tf_op jit(solution)/shard_map/all_to_all | solution.py:189
  18.8 2.1 copy-start.1
  86.4 14.1 %copy-start.10 = (f32[512]{0:T(512)S(1)}, f32[512]{0:T(512)}, u32[]{:S(2)}) copy-start(f32[512]{0:T(512)} %param.13) | copy-start | bytes 6148
  86.4 15.3 %copy-start.6 = (bf16[256,512]{1,0:T(8,128)(2,1)S(1)}, bf16[256,512]{1,0:T(8,128)(2,1)}, u32[]{:S(2)}) copy-start(bf16[256,512]{1,0:T(8,128)(2,1)} %param.14) | copy-start | bytes 786436
  103.3 30.9 %all-to-all-start.2 = ((bf16[8,256,512]{2,1,0:T(8,128)(2,1)}), bf16[8,256,512]{2,1,0:T(8,128)(2,1)S(1)}, u32[]{:S(2)}, u32[]{:S(2)}) async-start(bf16[8,256,512]{2,1,0:T(8,128)(2,1)} %broadcast_in_dim.12), calls=%async_computation.2 | async-start | bytes 4194304 | tf_op jit(solution)/shard_map/all_to_all | solution.py:220
  210.3 1.5 copy-start.2
  211.9 9.4 %copy-start.4 = (bf16[16,128,128]{2,1,0:T(8,128)(2,1)S(1)}, bf16[16,128,128]{2,1,0:T(8,128)(2,1)}, u32[]{:S(2)}) copy-start(bf16[16,128,128]{2,1,0:T(8,128)(2,1)} %bank_ref.3) | copy-start | bytes 1572868
  213.0 33.2 %all-to-all-start.5 = ((f32[32,5,512]{2,1,0:T(8,128)}), f32[32,5,512]{2,1,0:T(8,128)}, u32[]{:S(2)}, u32[]{:S(2)}) async-start(f32[32,5,512]{2,1,0:T(8,128)} %broadcast_in_dim.15), calls=%async_computation.5 | async-start | bytes 1048576 | tf_op jit(solution)/shard_map/all_to_all | solution.py:273
  232.6 1.9 copy-start.3
  246.1 14.0 %all-to-all-start.4 = ((bf16[8,256,128]{2,1,0:T(8,128)(2,1)}), bf16[8,256,128]{2,1,0:T(8,128)(2,1)S(1)}, u32[]{:S(2)}, u32[]{:S(2)}) async-start(bf16[8,256,128]{2,1,0:T(8,128)(2,1)} %bitcast.68), calls=%async_computation.4 | async-start | bytes 1048576 | tf_op jit(solution)/shard_map/all_to_all | solution.py:265
  260.1 1.6 copy-start.5
  261.7 30.7 %all-to-all-start.6 = ((f32[8,128,512]{2,1,0:T(8,128)}), f32[8,128,512]{2,1,0:T(8,128)S(1)}, u32[]{:S(2)}, u32[]{:S(2)}) async-start(f32[8,128,512]{2,1,0:T(8,128)} %broadcast_in_dim.16), calls=%async_computation.6 | async-start | bytes 4194304 | tf_op jit(solution)/shard_map/all_to_all | solution.py:276

commit v6 on v4

--- a/solution.py
+++ b/solution.py
@@ -96,6 +96,65 @@
         compiler_params=pltpu.CompilerParams(collective_id=0, has_side_effects=True),
         cost_estimate=_cost(cols.size, tile, 2 * bank.size + 6 * blocks.size + 4 * send.size),
     )(cols, banks, bank, blocks, send)
+
+
+def _exchange_kernel(domains, send_ref, recv_ref, send_sems, recv_sems, own_sem):
+    me = lax.axis_index("dom")
+    group = lax.axis_index("grp")
+    mesh_ids = pl.DeviceIdType.MESH
+
+    def remote(target, slot):
+        return pltpu.make_async_remote_copy(
+            src_ref=send_ref.at[target],
+            dst_ref=recv_ref.at[slot],
+            send_sem=send_sems.at[target],
+            recv_sem=recv_sems.at[slot],
+            device_id=(target, group),
+            device_id_type=mesh_ids,
+        )
+
+    barrier = pltpu.get_barrier_semaphore()
+
+    def greet(i, carry):
+        target = lax.rem(me + i, domains)
+        pl.semaphore_signal(barrier, 1, device_id=(target, group), device_id_type=mesh_ids)
+        return carry
+
+    lax.fori_loop(1, domains, greet, 0)
+    pl.semaphore_wait(barrier, domains - 1)
+
+    def send(i, carry):
+        remote(lax.rem(me + i, domains), me).start()
+        return carry
+
+    lax.fori_loop(1, domains, send, 0)
+    own = pltpu.make_async_copy(send_ref.at[me], recv_ref.at[me], own_sem)
+    own.start()
+    own.wait()
+
+    def finish(i, carry):
+        remote(lax.rem(me + i, domains), me).wait_send()
+        remote(me, lax.rem(me + domains - i, domains)).wait_recv()
+        return carry
+
+    lax.fori_loop(1, domains, finish, 0)
+
+
+def _exchange(send):
+    domains = send.shape[0]
+    return pl.pallas_call(
+        functools.partial(_exchange_kernel, domains),
+        out_shape=jax.ShapeDtypeStruct(send.shape, send.dtype),
+        in_specs=[pl.BlockSpec(memory_space=pl.ANY)],
+        out_specs=pl.BlockSpec(memory_space=pl.ANY),
+        scratch_shapes=[
+            pltpu.SemaphoreType.DMA((domains,)),
+            pltpu.SemaphoreType.DMA((domains,)),
+            pltpu.SemaphoreType.DMA,
+        ],
+        compiler_params=pltpu.CompilerParams(collective_id=1, has_side_effects=True),
+        cost_estimate=pl.CostEstimate(flops=0, transcendentals=0, bytes_accessed=4 * send.size),
+    )(send)
 
 
 def _bwd_local_kernel(cols, banks, bank_t_ref, grad_ref, acc_ref):
@@ -235,7 +294,7 @@
         halo_banks[0].astype(jnp.bfloat16)[:, :, None, None], (domains, slot_count, 8, narrow)
     )
     payload = jnp.concatenate([grad_blocks[rows_in], bank_rows], axis=2)
-    back_in = lax.all_to_all(payload, "dom", 0, 0, tiled=True)
+    back_in = _exchange(payload)
     banks_back = back_in[:, :, tile_size, 0].astype(jnp.int32)
     live_out = (outgoing >= 0).astype(jnp.int32).reshape(-1)
 

time: 291 us -> 303 us (1.041)
  Pallas kernels: 85.5 us -> 143 us
  blocking collectives: 65.2 us -> 42.9 us
  waiting for transfers between devices: 67.5 us -> 45.7 us
    pallas_call x0 -> x1, Pallas kernels: none -> 57.2 us  [_exchange(): pl.pallas_call(functools.partial(_exchange_kernel, domains), out_shape=ja...]
    all_to_all x1, waiting for transfers between devices: 49.3 us -> 10.1 us  [_dom_sum(): lax.all_to_all(y.reshape(domains, piece, width), 'dom', 0, 0, tiled=True)]
    all_to_all x1 -> x0, blocking collectives: 22.2 us -> none  [_dom_sum(): lax.all_to_all(y.reshape(domains, piece, width), 'dom', 0, 0, tiled=True)]
    all_to_all x1, waiting for transfers between devices: 1.69 us -> 23.9 us  [per_device(): lax.all_to_all(jnp.broadcast_to(summed[None, :narrow], (groups, narrow, s...]
    all_to_all x1, waiting for transfers between devices: 8.17 us -> 0.01 us  [_dom_sum(): lax.all_to_all(jnp.broadcast_to(z[None], (domains, piece, width)), 'dom',...]
    all_to_all x1, waiting for transfers between devices: 4.96 us -> 8.37 us  [per_device(): lax.all_to_all(grad_total.reshape(part_rows, narrow), 'grp', split_axis=0...]
    all_to_all x1, starting transfers between devices: 4.27 us -> 7.48 us  [per_device(): lax.all_to_all(grad_total.reshape(part_rows, narrow), 'grp', split_axis=0...]
  transfers between devices with their start and end apart: 5 -> 5, of which waited for: 5 -> 4; matrix products, arithmetic and copies ran while one was open for 9% -> 7% of each run, Pallas kernels for 6% -> 25%
where the time goes in v6:
time: 303 us; the launch traced here: 302 us
  Pallas kernels  143 us (47%)
  waiting for transfers between devices  45.7 us (15%)
  blocking collectives  42.9 us (14%)
  starting transfers between devices  33.8 us (11%)
  local copies, waits for them, and re-layouts  21.4 us (7%)
  other arithmetic  10.7 us (4%)
  matrix products  3.14 us (1%)
    pallas_call x1, Pallas kernels, _fwd_exchange(): pl.pallas_call(functools.partial(_fwd_exchange_kernel, domains), out_shap...  58.3 us
    pallas_call x1, Pallas kernels, _exchange(): pl.pallas_call(functools.partial(_exchange_kernel, domains), out_shape=ja...  57.2 us
    all_to_all x1, blocking collectives, per_device(): lax.all_to_all(jnp.broadcast_to(grad_pre[None], (groups,) + grad_pre.shap...  30.1 us
    all_to_all x1, waiting for transfers between devices, per_device(): lax.all_to_all(jnp.broadcast_to(summed[None, :narrow], (groups, narrow, s...  23.9 us
    pallas_call x2, Pallas kernels, _halo(): pl.pallas_call(_halo_kernel, out_shape=jax.ShapeDtypeStruct((n, tile, wid...  20.6 us
    all_to_all x1, blocking collectives, per_device(): lax.all_to_all(agg_narrow, 'grp', split_axis=0, concat_axis=1, tiled=True)  12.8 us
    all_to_all x1, waiting for transfers between devices, _dom_sum(): lax.all_to_all(y.reshape(domains, piece, width), 'dom', 0, 0, tiled=True)  10.1 us
    all_to_all x1, waiting for transfers between devices, per_device(): lax.all_to_all(grad_total.reshape(part_rows, narrow), 'grp', split_axis=0...  8.37 us
  transfers between devices with their start and end apart: 5, of which 4 were waited for; matrix products, arithmetic and copies ran while one was open for 7% of the time, Pallas kernels for 25%

profile of v6, /device:TPU:1, one launch (start us, length us, event | category | flops | bytes accessed | tf_op | source)
XLA Modules:
  0.0 301.5 jit_solution(15697912467449586036)
XLA Ops:
  0.7 2.0 copy_bitcast_fusion.1
  2.7 6.6 %all-to-all-start = ((bf16[256,8,128]{2,0,1:T(8,128)(2,1)}), bf16[256,8,128]{2,0,1:T(8,128)(2,1)S(1)}, u32[]{:S(2)}, u32[]{:S(2)}) async-start(bf16[256,8,128]{2,0,1:T(8,128)(2,1)} %copy_bitcast_fusion.1), calls=%async_computation | async-start | bytes 1048576 | tf_op jit(solution)/shard_map/all_to_all | solution.py:248
  10.0 2.6 compare_select_fusion.1
  15.5 3.3 %all-to-all-done = bf16[256,8,128]{2,0,1:T(8,128)(2,1)S(1)} async-done(((bf16[256,8,128]{2,0,1:T(8,128)(2,1)}), bf16[256,8,128]{2,0,1:T(8,128)(2,1)S(1)}, u32[]{:S(2)}, u32[]{:S(2)}) %all-to-all-start) | async-done | bytes 524320 | tf_op jit(solution)/shard_map/all_to_all | solution.py:248
  18.8 2.1 gather_fusion
  21.0 58.3 %shard_map.138 = (f32[16,128,128]{2,1,0:T(8,128)}, bf16[32,2,128,128]{3,2,1,0:T(8,128)(2,1)}) custom-call(s32[16,16]{1,0:T(8,128)} %bitcast.70, s32[16,16]{1,0:T(8,128)} %bitcast.72, bf16[16,128,128]{2,1,0:T(8,128)(2,1)} %bank_ref.3, bf16[16,128,128]{2,1,0:T(8,128)(2,1)} %bitcast.54, bf16[32,2,128,128]{3,2,1,0:T(8,128)(2,1)} %bitcast.66), custom_call_target="tpu_custom_call" | custom-call | flops 1073741824 | bytes 6291456 | tf_op jit(solution)/shard_map/pallas_call | solution.py:83
  79.2 9.0 %shard_map.139 = bf16[16,128,128]{2,1,0:T(8,128)(2,1)} custom-call(s32[64]{0:T(128)} %reshape_squeeze.6.dest, s32[64]{0:T(128)} %reshape_squeeze.7.banks, s32[64]{0:T(128)} %reshape.141.live, bf16[16,128,128]{2,1,0:T(8,128)(2,1)} %bank_ref.3, f32[16,128,128]{2,1,0:T(8,128)} %get-tuple-element.6.acc_in, bf16[64,128,128]{2,1,0:T(8,128)(2,1)} %bitcast.61), custom_call_target="tpu_custom_call" | custom-call | flops 268435456 | bytes 4194304 | tf_op jit(solution)/shard_map/pallas_call | solution.py:207
  89.5 12.8 %all_to_all.74 = bf16[8,256,128]{1,2,0:T(8,128)(2,1)S(1)} all-to-all(bf16[8,256,128]{1,2,0:T(8,128)(2,1)S(1)} %copy.40), channel_id=1, replica_groups=mesh['dom'=32,'grp'=8] {'grp'}, dimensions={0} | all-to-all | bytes 1048576 | tf_op jit(solution)/shard_map/all_to_all | solution.py:275
  103.8 30.1 %all_to_all.75 = bf16[8,256,512]{2,1,0:T(8,128)(2,1)S(1)} all-to-all(bf16[8,256,512]{2,1,0:T(8,128)(2,1)S(1)} %broadcast_in_dim.12), channel_id=1, replica_groups=mesh['dom'=32,'grp'=8] {'grp'}, dimensions={0} | all-to-all | bytes 4194304 | tf_op jit(solution)/shard_map/all_to_all | solution.py:279
  135.6 7.2 %all-to-all-start.4 = ((f32[32,5,512]{2,1,0:T(8,128)}), f32[32,5,512]{2,1,0:T(8,128)}, u32[]{:S(2)}, u32[]{:S(2)}) async-start(f32[32,5,512]{2,1,0:T(8,128)} %reshape.139), calls=%async_computation.4 | async-start | bytes 1048576 | tf_op jit(solution)/shard_map/all_to_all | solution.py:222
  142.8 2.1 copy.45
  146.6 10.1 %all-to-all-done.4 = f32[32,5,512]{2,1,0:T(8,128)} async-done(((f32[32,5,512]{2,1,0:T(8,128)}), f32[32,5,512]{2,1,0:T(8,128)}, u32[]{:S(2)}, u32[]{:S(2)}) %all-to-all-start.4) | async-done | bytes 327712 | tf_op jit(solution)/shard_map/all_to_all | solution.py:222
  158.7 8.1 %all-to-all-start.5 = ((f32[32,5,512]{2,1,0:T(8,128)}), f32[32,5,512]{2,1,0:T(8,128)}, u32[]{:S(2)}, u32[]{:S(2)}) async-start(f32[32,5,512]{2,1,0:T(8,128)} %broadcast_in_dim.15), calls=%async_computation.5 | async-start | bytes 1048576 | tf_op jit(solution)/shard_map/all_to_all | solution.py:223
  168.3 2.0 gather_fusion.1
  172.0 57.2 %shard_map.140 = bf16[32,2,136,128]{3,2,1,0:T(8,128)(2,1)} custom-call(bf16[32,2,136,128]{3,2,1,0:T(8,128)(2,1)} %pad_maximum_fusion.send_ref), custom_call_target="tpu_custom_call" | custom-call | bytes 4456448 | tf_op jit(solution)/shard_map/pallas_call | solution.py:145
  229.2 2.1 convert_reduce_fusion.1
  231.9 7.1 %shard_map.141.acc_in = f32[16,128,128]{2,1,0:T(8,128)} custom-call(s32[16,16]{1,0:T(8,128)} %bitcast.71, s32[16,16]{1,0:T(8,128)} %bitcast.73, bf16[16,128,128]{2,1,0:T(8,128)(2,1)} %bitcast.62, bf16[16,128,128]{2,1,0:T(8,128)(2,1)} %bitcast.56), custom_call_target="tpu_custom_call" | custom-call | flops 1073741824 | bytes 2097152 | tf_op jit(solution)/shard_map/pallas_call | solution.py:196
  239.0 11.6 %shard_map.142 = bf16[16,128,128]{2,1,0:T(8,128)(2,1)} custom-call(s32[64]{0:T(128)} %reshape.134.dest, s32[64]{0:T(128)} %reshape.142.banks, s32[64]{0:T(128)} %reshape.143.live, bf16[16,128,128]{2,1,0:T(8,128)(2,1)} %bitcast.63, f32[16,128,128]{2,1,0:T(8,128)} %shard_map.141.acc_in, bf16[64,136,128]{2,1,0:T(8,128)(2,1)} %bitcast.57), custom_call_target="tpu_custom_call" | custom-call | flops 268435456 | bytes 4325376 | tf_op jit(solution)/shard_map/pallas_call | solution.py:207
  250.6 7.5 %all-to-all-start.3 = ((bf16[8,256,128]{2,1,0:T(8,128)(2,1)}), bf16[8,256,128]{2,1,0:T(8,128)(2,1)S(1)}, u32[]{:S(2)}, u32[]{:S(2)}) async-start(bf16[8,256,128]{2,1,0:T(8,128)(2,1)} %bitcast.64), calls=%async_computation.3 | async-start | bytes 1048576 | tf_op jit(solution)/shard_map/all_to_all | solution.py:310
  259.2 8.4 %all-to-all-done.3 = bf16[8,256,128]{2,1,0:T(8,128)(2,1)S(1)} async-done(((bf16[8,256,128]{2,1,0:T(8,128)(2,1)}), bf16[8,256,128]{2,1,0:T(8,128)(2,1)S(1)}, u32[]{:S(2)}, u32[]{:S(2)}) %all-to-all-start.3) | async-done | bytes 524320 | tf_op jit(solution)/shard_map/all_to_all | solution.py:310
  269.2 4.4 %all-to-all-start.6 = ((f32[8,128,512]{2,1,0:T(8,128)}), f32[8,128,512]{2,1,0:T(8,128)S(1)}, u32[]{:S(2)}, u32[]{:S(2)}) async-start(f32[8,128,512]{2,1,0:T(8,128)} %broadcast_in_dim.16), calls=%async_computation.6 | async-start | bytes 4194304 | tf_op jit(solution)/shard_map/all_to_all | solution.py:319
  273.6 1.9 copy_bitcast_fusion
  276.1 23.9 %all-to-all-done.6 = f32[8,128,512]{2,1,0:T(8,128)S(1)} async-done(((f32[8,128,512]{2,1,0:T(8,128)}), f32[8,128,512]{2,1,0:T(8,128)S(1)}, u32[]{:S(2)}, u32[]{:S(2)}) %all-to-all-start.6) | async-done | bytes 2097184 | tf_op jit(solution)/shard_map/all_to_all | solution.py:319
  299.9 1.6 broadcast_multiply_fusion
  (59 shorter events, 18.8 us)
Async XLA Ops:
  0.6 101.7 %copy-start = (bf16[1024,512]{1,0:T(8,128)(2,1)S(1)}, bf16[1024,512]{1,0:T(8,128)(2,1)}, u32[]{:S(2)}) copy-start(bf16[1024,512]{1,0:T(8,128)(2,1)} %param.12) | copy-start | bytes 3145732
  0.6 8.7 %copy-start.7 = (s32[1,32,2]{1,2,0:T(2,128)S(1)}, s32[1,32,2]{1,2,0:T(2,128)}, u32[]{:S(2)}) copy-start(s32[1,32,2]{1,2,0:T(2,128)} %param.20) | copy-start | bytes 772
  0.7 8.8 %copy-start.6 = (s32[1,4]{1,0:T(1,128)S(1)}, s32[1,4]{1,0:T(1,128)}, u32[]{:S(2)}) copy-start(s32[1,4]{1,0:T(1,128)} %param.18) | copy-start | bytes 52
  0.7 9.4 %copy-start.5 = (s32[32,32,2]{1,2,0:T(2,128)S(1)}, s32[32,32,2]{1,2,0:T(2,128)}, u32[]{:S(2)}) copy-start(s32[32,32,2]{1,2,0:T(2,128)} %param.19) | copy-start | bytes 24580
  0.7 14.1 %copy-start.9 = (s32[1,32,2]{1,2,0:T(2,128)S(1)}, s32[1,32,2]{1,2,0:T(2,128)}, u32[]{:S(2)}) copy-start(s32[1,32,2]{1,2,0:T(2,128)} %param.21) | copy-start | bytes 772
  2.7 16.1 %all-to-all-start = ((bf16[256,8,128]{2,0,1:T(8,128)(2,1)}), bf16[256,8,128]{2,0,1:T(8,128)(2,1)S(1)}, u32[]{:S(2)}, u32[]{:S(2)}) async-start(bf16[256,8,128]{2,0,1:T(8,128)(2,1)} %copy_bitcast_fusion.1), calls=%async_computation | async-start | bytes 1048576 | tf_op jit(solution)/shard_map/all_to_all | solution.py:248
  18.8 2.1 copy-start.1
  88.2 14.1 %copy-start.8 = (f32[512]{0:T(512)S(1)}, f32[512]{0:T(512)}, u32[]{:S(2)}) copy-start(f32[512]{0:T(512)} %param.13) | copy-start | bytes 6148
  88.2 15.3 %copy-start.4 = (bf16[256,512]{1,0:T(8,128)(2,1)S(1)}, bf16[256,512]{1,0:T(8,128)(2,1)}, u32[]{:S(2)}) copy-start(bf16[256,512]{1,0:T(8,128)(2,1)} %param.14) | copy-start | bytes 786436
  103.8 30.1 %copy-start.2 = (bf16[16,128,128]{2,1,0:T(8,128)(2,1)S(1)}, bf16[16,128,128]{2,1,0:T(8,128)(2,1)}, u32[]{:S(2)}) copy-start(bf16[16,128,128]{2,1,0:T(8,128)(2,1)} %shard_map.139) | copy-start | bytes 1572868
  135.6 21.2 %all-to-all-start.4 = ((f32[32,5,512]{2,1,0:T(8,128)}), f32[32,5,512]{2,1,0:T(8,128)}, u32[]{:S(2)}, u32[]{:S(2)}) async-start(f32[32,5,512]{2,1,0:T(8,128)} %reshape.139), calls=%async_computation.4 | async-start | bytes 1048576 | tf_op jit(solution)/shard_map/all_to_all | solution.py:222
  158.7 91.9 %all-to-all-start.5 = ((f32[32,5,512]{2,1,0:T(8,128)}), f32[32,5,512]{2,1,0:T(8,128)}, u32[]{:S(2)}, u32[]{:S(2)}) async-start(f32[32,5,512]{2,1,0:T(8,128)} %broadcast_in_dim.15), calls=%async_computation.5 | async-start | bytes 1048576 | tf_op jit(solution)/shard_map/all_to_all | solution.py:223
  250.6 17.0 %all-to-all-start.3 = ((bf16[8,256,128]{2,1,0:T(8,128)(2,1)}), bf16[8,256,128]{2,1,0:T(8,128)(2,1)S(1)}, u32[]{:S(2)}, u32[]{:S(2)}) async-start(bf16[8,256,128]{2,1,0:T(8,128)(2,1)} %bitcast.64), calls=%async_computation.3 | async-start | bytes 1048576 | tf_op jit(solution)/shard_map/all_to_all | solution.py:310
  267.6 1.6 copy-start.3
  269.2 30.7 %all-to-all-start.6 = ((f32[8,128,512]{2,1,0:T(8,128)}), f32[8,128,512]{2,1,0:T(8,128)S(1)}, u32[]{:S(2)}, u32[]{:S(2)}) async-start(f32[8,128,512]{2,1,0:T(8,128)} %broadcast_in_dim.16), calls=%async_computation.6 | async-start | bytes 4194304 | tf_op jit(solution)/shard_map/all_to_all | solution.py:319

commit v7 on v4

--- a/solution.py
+++ b/solution.py
@@ -256,19 +256,27 @@
         tiled=True,
     )
     norm_scale = float(rows_here * groups * domains) ** (-0.5)
-    summed = _dom_sum(jnp.concatenate([weight_part, bias_part[None]], axis=0))
-    weight_total = lax.all_to_all(
-        jnp.broadcast_to(summed[None, :narrow], (groups, narrow, summed.shape[1])),
-        "grp",
+    partial = jnp.concatenate([weight_part, bias_part[None]], axis=0)
+    kept_rows, width = partial.shape
+    piece = -(-kept_rows // domains)
+    padded = jnp.pad(partial, ((0, piece * domains - kept_rows), (0, 0)))
+    reduced = lax.all_to_all(
+        padded.reshape(domains, piece, width), "dom", 0, 0, tiled=True
+    ).sum(0)
+    gathered = lax.all_to_all(
+        jnp.broadcast_to(reduced[None], (domains * groups, piece, width)),
+        ("dom", "grp"),
         0,
         0,
         tiled=True,
-    ).reshape(groups * narrow, summed.shape[1])
+    ).reshape(domains, groups, piece, width)
+    slices = jnp.swapaxes(gathered, 0, 1).reshape(groups, domains * piece, width)
+    weight_total = slices[:, :narrow].reshape(groups * narrow, width)
     return (
         activations,
         grad_nodes,
         weight_total * norm_scale,
-        summed[narrow] * norm_scale,
+        slices[0, narrow] * norm_scale,
     )
 
 

time: 291 us -> 368 us (1.26)
  waiting for transfers between devices: 67.5 us -> 184 us
  blocking collectives: 65.2 us -> 12.8 us
  starting transfers between devices: 32.9 us -> 48.7 us
  Pallas kernels: 85.5 us -> 78.2 us
  local copies, waits for them, and re-layouts: 22.2 us -> 28.6 us
    all_to_all x2 -> x3, waiting for transfers between devices: 9.87 us -> 123 us  [the longest x1 96.5 us: per_device(): lax.all_to_all(jnp.broadcast_to(reduced[None], (domains * groups, piece,...]
    all_to_all x2 -> x0, blocking collectives: 52.3 us -> none  [the longest x1 30.1 us: per_device(): lax.all_to_all(jnp.broadcast_to(grad_pre[None], (groups,) + grad_pre.shap...]
    all_to_all x2 -> x3, starting transfers between devices: 14.1 us -> 30.2 us  [the longest x1 18.5 us: per_device(): lax.all_to_all(jnp.broadcast_to(reduced[None], (domains * groups, piece,...]
    pallas_call x2, Pallas kernels: 20.2 us -> 12.9 us  [_halo(): pl.pallas_call(_halo_kernel, out_shape=jax.ShapeDtypeStruct((n, tile, wid...]
    transpose x0 -> x1, local copies, waits for them, and re-layouts: none -> 4.57 us  [per_device(): jnp.swapaxes(gathered, 0, 1).reshape(groups, domains * piece, width)]
    all_to_all x1, waiting for transfers between devices: 4.96 us -> 9.45 us  [per_device(): lax.all_to_all(grad_total.reshape(part_rows, narrow), 'grp', split_axis=0...]
  transfers between devices with their start and end apart: 5 -> 6, of which waited for: 5 -> 5; matrix products, arithmetic and copies ran while one was open for 9% -> 4% of each run, Pallas kernels for 6% -> 3%
where the time goes in v7:
time: 368 us; the launch traced here: 366 us
  waiting for transfers between devices  184 us (50%)
  Pallas kernels  78.2 us (21%)
  starting transfers between devices  48.7 us (13%)
  local copies, waits for them, and re-layouts  28.6 us (8%)
  blocking collectives  12.8 us (3%)
  other arithmetic  9.85 us (3%)
    all_to_all x1, waiting for transfers between devices, per_device(): lax.all_to_all(jnp.broadcast_to(reduced[None], (domains * groups, piece,...  96.5 us
    pallas_call x1, Pallas kernels, _fwd_exchange(): pl.pallas_call(functools.partial(_fwd_exchange_kernel, domains), out_shap...  58.3 us
    all_to_all x1, waiting for transfers between devices, per_device(): back_in = lax.all_to_all(payload, 'dom', 0, 0, tiled=True)  49 us
    all_to_all x1, waiting for transfers between devices, per_device(): lax.all_to_all(jnp.broadcast_to(grad_pre[None], (groups,) + grad_pre.shap...  26 us
    all_to_all x1, starting transfers between devices, per_device(): lax.all_to_all(jnp.broadcast_to(reduced[None], (domains * groups, piece,...  18.5 us
    pallas_call x2, Pallas kernels, _halo(): pl.pallas_call(_halo_kernel, out_shape=jax.ShapeDtypeStruct((n, tile, wid...  12.9 us
    all_to_all x1, blocking collectives, per_device(): lax.all_to_all(agg_narrow, 'grp', split_axis=0, concat_axis=1, tiled=True)  12.8 us
    all_to_all x1, waiting for transfers between devices, per_device(): lax.all_to_all(grad_total.reshape(part_rows, narrow), 'grp', split_axis=0...  9.45 us
  transfers between devices with their start and end apart: 6, of which 5 were waited for; matrix products, arithmetic and copies ran while one was open for 4% of the time, Pallas kernels for 3%

profile of v7, /device:TPU:1, one launch (start us, length us, event | category | flops | bytes accessed | tf_op | source)
XLA Modules:
  0.0 366.5 jit_solution(4824711979821207470)
XLA Ops:
  2.7 6.6 %all-to-all-start = ((bf16[256,8,128]{2,0,1:T(8,128)(2,1)}), bf16[256,8,128]{2,0,1:T(8,128)(2,1)S(1)}, u32[]{:S(2)}, u32[]{:S(2)}) async-start(bf16[256,8,128]{2,0,1:T(8,128)(2,1)} %copy_bitcast_fusion.1), calls=%async_computation | async-start | bytes 1048576 | tf_op jit(solution)/shard_map/all_to_all | solution.py:189
  10.0 2.6 compare_select_fusion.1
  15.5 3.3 all-to-all-done
  18.8 2.1 gather_fusion
  21.0 58.3 %shard_map.138 = (f32[16,128,128]{2,1,0:T(8,128)}, bf16[32,2,128,128]{3,2,1,0:T(8,128)(2,1)}) custom-call(s32[16,16]{1,0:T(8,128)} %bitcast.75, s32[16,16]{1,0:T(8,128)} %bitcast.77, bf16[16,128,128]{2,1,0:T(8,128)(2,1)} %bank_ref.3, bf16[16,128,128]{2,1,0:T(8,128)(2,1)} %bitcast.58, bf16[32,2,128,128]{3,2,1,0:T(8,128)(2,1)} %bitcast.71), custom_call_target="tpu_custom_call" | custom-call | flops 1073741824 | bytes 6291456 | tf_op jit(solution)/shard_map/pallas_call | solution.py:83
  79.2 7.4 %shard_map.139 = bf16[16,128,128]{2,1,0:T(8,128)(2,1)} custom-call(s32[64]{0:T(128)} %reshape_squeeze.6.dest, s32[64]{0:T(128)} %reshape_squeeze.7.banks, s32[64]{0:T(128)} %reshape.144.live, bf16[16,128,128]{2,1,0:T(8,128)(2,1)} %bank_ref.3, f32[16,128,128]{2,1,0:T(8,128)} %get-tuple-element.6.acc_in, bf16[64,128,128]{2,1,0:T(8,128)(2,1)} %bitcast.66), custom_call_target="tpu_custom_call" | custom-call | flops 268435456 | bytes 4194304 | tf_op jit(solution)/shard_map/pallas_call | solution.py:148
  87.9 12.8 %all_to_all.74 = bf16[8,256,128]{1,2,0:T(8,128)(2,1)S(1)} all-to-all(bf16[8,256,128]{1,2,0:T(8,128)(2,1)S(1)} %copy.74), channel_id=1, replica_groups=mesh['dom'=32,'grp'=8] {'grp'}, dimensions={0} | all-to-all | bytes 1048576 | tf_op jit(solution)/shard_map/all_to_all | solution.py:216
  103.5 4.5 %all-to-all-start.2 = ((bf16[8,256,512]{2,1,0:T(8,128)(2,1)}), bf16[8,256,512]{2,1,0:T(8,128)(2,1)S(1)}, u32[]{:S(2)}, u32[]{:S(2)}) async-start(bf16[8,256,512]{2,1,0:T(8,128)(2,1)} %broadcast_in_dim.10), calls=%async_computation.2 | async-start | bytes 4194304 | tf_op jit(solution)/shard_map/all_to_all | solution.py:220
  108.3 26.0 %all-to-all-done.2 = bf16[8,256,512]{2,1,0:T(8,128)(2,1)S(1)} async-done(((bf16[8,256,512]{2,1,0:T(8,128)(2,1)}), bf16[8,256,512]{2,1,0:T(8,128)(2,1)S(1)}, u32[]{:S(2)}, u32[]{:S(2)}) %all-to-all-start.2) | async-done | bytes 2097184 | tf_op jit(solution)/shard_map/all_to_all | solution.py:220
  135.9 3.2 gather_fusion.1
  139.2 3.1 pad_maximum_fusion
  142.3 7.2 %all-to-all-start.3 = ((bf16[32,2,136,128]{3,2,1,0:T(8,128)(2,1)}), bf16[32,2,136,128]{3,2,1,0:T(8,128)(2,1)}, u32[]{:S(2)}, u32[]{:S(2)}) async-start(bf16[32,2,136,128]{3,2,1,0:T(8,128)(2,1)} %pad_maximum_fusion), calls=%async_computation.3 | async-start | bytes 4456448 | tf_op jit(solution)/shard_map/all_to_all | solution.py:238
  152.0 49.0 %all-to-all-done.3 = bf16[32,2,136,128]{3,2,1,0:T(8,128)(2,1)} async-done(((bf16[32,2,136,128]{3,2,1,0:T(8,128)(2,1)}), bf16[32,2,136,128]{3,2,1,0:T(8,128)(2,1)}, u32[]{:S(2)}, u32[]{:S(2)}) %all-to-all-start.3) | async-done | bytes 2228256 | tf_op jit(solution)/shard_map/all_to_all | solution.py:238
  201.0 7.1 %all-to-all-start.5 = ((f32[32,5,512]{2,1,0:T(8,128)}), f32[32,5,512]{2,1,0:T(8,128)S(1)}, u32[]{:S(2)}, u32[]{:S(2)}) async-start(f32[32,5,512]{2,1,0:T(8,128)} %reshape.141), calls=%async_computation.5 | async-start | bytes 1048576 | tf_op jit(solution)/shard_map/all_to_all | solution.py:263
  210.6 7.0 %shard_map.140.acc_in = f32[16,128,128]{2,1,0:T(8,128)} custom-call(s32[16,16]{1,0:T(8,128)} %bitcast.76, s32[16,16]{1,0:T(8,128)} %bitcast.78, bf16[16,128,128]{2,1,0:T(8,128)(2,1)} %bitcast.68, bf16[16,128,128]{2,1,0:T(8,128)(2,1)} %bitcast.60), custom_call_target="tpu_custom_call" | custom-call | flops 1073741824 | bytes 2097152 | tf_op jit(solution)/shard_map/pallas_call | solution.py:137
  217.7 2.1 fusion.2
  220.5 5.5 %shard_map.141 = bf16[16,128,128]{2,1,0:T(8,128)(2,1)} custom-call(s32[64]{0:T(128)} %reshape.136.dest, s32[64]{0:T(128)} %reshape.145.banks, s32[64]{0:T(128)} %reshape.146.live, bf16[16,128,128]{2,1,0:T(8,128)(2,1)} %bitcast.69, f32[16,128,128]{2,1,0:T(8,128)} %shard_map.140.acc_in, bf16[64,136,128]{2,1,0:T(8,128)(2,1)} %bitcast.21.blocks_ref), custom_call_target="tpu_custom_call" | custom-call | flops 268435456 | bytes 4325376 | tf_op jit(solution)/shard_map/pallas_call | solution.py:148
  226.0 4.7 %all-to-all-start.4 = ((bf16[8,256,128]{2,1,0:T(8,128)(2,1)}), bf16[8,256,128]{2,1,0:T(8,128)(2,1)S(1)}, u32[]{:S(2)}, u32[]{:S(2)}) async-start(bf16[8,256,128]{2,1,0:T(8,128)(2,1)} %bitcast.67), calls=%async_computation.4 | async-start | bytes 1048576 | tf_op jit(solution)/shard_map/all_to_all | solution.py:251
  230.8 9.4 %all-to-all-done.4 = bf16[8,256,128]{2,1,0:T(8,128)(2,1)S(1)} async-done(((bf16[8,256,128]{2,1,0:T(8,128)(2,1)}), bf16[8,256,128]{2,1,0:T(8,128)(2,1)S(1)}, u32[]{:S(2)}, u32[]{:S(2)}) %all-to-all-start.4) | async-done | bytes 524320 | tf_op jit(solution)/shard_map/all_to_all | solution.py:251
  240.2 2.5 broadcast_in_dim.13
  242.7 18.5 %all-to-all-start.6 = ((f32[256,5,512]{2,1,0:T(8,128)}), f32[256,5,512]{2,1,0:T(8,128)}, u32[]{:S(2)}, u32[]{:S(2)}) async-start(f32[256,5,512]{2,1,0:T(8,128)} %broadcast_in_dim.13), calls=%async_computation.6 | async-start | bytes 8388608 | tf_op jit(solution)/shard_map/all_to_all | solution.py:266
  262.1 96.5 %all-to-all-done.6 = f32[256,5,512]{2,1,0:T(8,128)} async-done(((f32[256,5,512]{2,1,0:T(8,128)}), f32[256,5,512]{2,1,0:T(8,128)}, u32[]{:S(2)}, u32[]{:S(2)}) %all-to-all-start.6) | async-done | bytes 2621472 | tf_op jit(solution)/shard_map/all_to_all | solution.py:266
  358.6 4.6 %copy.82 = f32[8,32,5,512]{3,0,2,1:T(8,128)S(1)} copy(f32[8,32,5,512]{3,2,0,1:T(8,128)} %bitcast.28) | data formatting | bytes 5242880 | tf_op jit(solution)/shard_map/transpose | solution.py:273
  364.0 2.5 copy.83
  (58 shorter events, 18.9 us)
Async XLA Ops:
  0.6 100.1 %copy-start = (bf16[1024,512]{1,0:T(8,128)(2,1)S(1)}, bf16[1024,512]{1,0:T(8,128)(2,1)}, u32[]{:S(2)}) copy-start(bf16[1024,512]{1,0:T(8,128)(2,1)} %param.12) | copy-start | bytes 3145732
  0.6 8.7 %copy-start.7 = (s32[1,32,2]{1,2,0:T(2,128)S(1)}, s32[1,32,2]{1,2,0:T(2,128)}, u32[]{:S(2)}) copy-start(s32[1,32,2]{1,2,0:T(2,128)} %param.20) | copy-start | bytes 772
  0.7 8.8 %copy-start.6 = (s32[1,4]{1,0:T(1,128)S(1)}, s32[1,4]{1,0:T(1,128)}, u32[]{:S(2)}) copy-start(s32[1,4]{1,0:T(1,128)} %param.18) | copy-start | bytes 52
  0.7 9.4 %copy-start.5 = (s32[32,32,2]{1,2,0:T(2,128)S(1)}, s32[32,32,2]{1,2,0:T(2,128)}, u32[]{:S(2)}) copy-start(s32[32,32,2]{1,2,0:T(2,128)} %param.19) | copy-start | bytes 24580
  0.7 14.1 %copy-start.9 = (s32[1,32,2]{1,2,0:T(2,128)S(1)}, s32[1,32,2]{1,2,0:T(2,128)}, u32[]{:S(2)}) copy-start(s32[1,32,2]{1,2,0:T(2,128)} %param.21) | copy-start | bytes 772
  2.7 16.1 %all-to-all-start = ((bf16[256,8,128]{2,0,1:T(8,128)(2,1)}), bf16[256,8,128]{2,0,1:T(8,128)(2,1)S(1)}, u32[]{:S(2)}, u32[]{:S(2)}) async-start(bf16[256,8,128]{2,0,1:T(8,128)(2,1)} %copy_bitcast_fusion.1), calls=%async_computation | async-start | bytes 1048576 | tf_op jit(solution)/shard_map/all_to_all | solution.py:189
  18.8 2.1 copy-start.1
  86.6 14.1 %copy-start.8 = (f32[512]{0:T(512)S(1)}, f32[512]{0:T(512)}, u32[]{:S(2)}) copy-start(f32[512]{0:T(512)} %param.13) | copy-start | bytes 6148
  86.6 15.3 %copy-start.4 = (bf16[256,512]{1,0:T(8,128)(2,1)S(1)}, bf16[256,512]{1,0:T(8,128)(2,1)}, u32[]{:S(2)}) copy-start(bf16[256,512]{1,0:T(8,128)(2,1)} %param.14) | copy-start | bytes 786436
  103.5 30.9 %all-to-all-start.2 = ((bf16[8,256,512]{2,1,0:T(8,128)(2,1)}), bf16[8,256,512]{2,1,0:T(8,128)(2,1)S(1)}, u32[]{:S(2)}, u32[]{:S(2)}) async-start(bf16[8,256,512]{2,1,0:T(8,128)(2,1)} %broadcast_in_dim.10), calls=%async_computation.2 | async-start | bytes 4194304 | tf_op jit(solution)/shard_map/all_to_all | solution.py:220
  142.3 58.7 %all-to-all-start.3 = ((bf16[32,2,136,128]{3,2,1,0:T(8,128)(2,1)}), bf16[32,2,136,128]{3,2,1,0:T(8,128)(2,1)}, u32[]{:S(2)}, u32[]{:S(2)}) async-start(bf16[32,2,136,128]{3,2,1,0:T(8,128)(2,1)} %pad_maximum_fusion), calls=%async_computation.3 | async-start | bytes 4456448 | tf_op jit(solution)/shard_map/all_to_all | solution.py:238
  149.5 1.0 copy-start.2
  151.1 57.1 %copy-start.3 = (bf16[16,128,128]{2,1,0:T(8,128)(2,1)S(1)}, bf16[16,128,128]{2,1,0:T(8,128)(2,1)}, u32[]{:S(2)}) copy-start(bf16[16,128,128]{2,1,0:T(8,128)(2,1)} %bank_ref.3) | copy-start | bytes 1572868
  201.0 25.0 %all-to-all-start.5 = ((f32[32,5,512]{2,1,0:T(8,128)}), f32[32,5,512]{2,1,0:T(8,128)S(1)}, u32[]{:S(2)}, u32[]{:S(2)}) async-start(f32[32,5,512]{2,1,0:T(8,128)} %reshape.141), calls=%async_computation.5 | async-start | bytes 1048576 | tf_op jit(solution)/shard_map/all_to_all | solution.py:263
  226.0 14.2 %all-to-all-start.4 = ((bf16[8,256,128]{2,1,0:T(8,128)(2,1)}), bf16[8,256,128]{2,1,0:T(8,128)(2,1)S(1)}, u32[]{:S(2)}, u32[]{:S(2)}) async-start(bf16[8,256,128]{2,1,0:T(8,128)(2,1)} %bitcast.67), calls=%async_computation.4 | async-start | bytes 1048576 | tf_op jit(solution)/shard_map/all_to_all | solution.py:251
  242.7 115.8 %all-to-all-start.6 = ((f32[256,5,512]{2,1,0:T(8,128)}), f32[256,5,512]{2,1,0:T(8,128)}, u32[]{:S(2)}, u32[]{:S(2)}) async-start(f32[256,5,512]{2,1,0:T(8,128)} %broadcast_in_dim.13), calls=%async_computation.6 | async-start | bytes 8388608 | tf_op jit(solution)/shard_map/all_to_all | solution.py:266
